TPU v7x, 32 devices: a whole 2x2x4 slice. The times are simulated.
32 devices in a mesh: req: 16 (over z, x, core), tp: 2 (over y).
Axes of the slice: x: 2, y: 2, z: 4, core: 2. Of those that a mesh axis runs over, the one named last changes fastest.
Arguments:
- queries: bfloat16 [2048, 16, 192], P('req', 'tp'), may hold values from -160 to 160
- stretch_cache: bfloat16 [2048, 576], P('req'), may hold values from -6 to 6
- prefix_pool: bfloat16 [192, 64, 576], P('req'), may hold values from -6 to 6
- page_table: int32 [16, 12], P('req'), may hold values from 0 to 11, each once within a row
- prefix_len: int32 [16], replicated, may hold values from 1 to 768, 6144 in all
- prompt_cache: bfloat16 [2, 256, 576], P(None, 'req'), may hold values from -6 to 6
- prompt_len: int32 [2], replicated, may hold values from 1 to 256, 384 in all
- group_ids: int32 [16], replicated, may hold values from 0 to 1
- absorb_weight: bfloat16 [16, 128, 512], P('tp'), may hold values from -0.5 to 0.5
- value_weight: bfloat16 [16, 512, 128], P('tp'), may hold values from -1 to 1
- out_weight: bfloat16 [2048, 2048], P('tp'), may hold values from -0.125 to 0.125
- residual: bfloat16 [2048, 2048], P('req', 'tp'), may hold values from -20 to 20
- norm_gain: bfloat16 [2048], P('tp'), may hold values from 0.099609375 to 1.8984375
- routes: int32 [2048, 6], P('req'), may hold values from 0 to 15, all different within a row; in each aligned block of 128 rows (0 to 127, 128 to 255, ...) at most 64 rows name the same one
- route_weight: float32 [2048, 6], P('req'), may hold values from 0.05 to 0.45
- gate_weight: bfloat16 [16, 2048, 1408], P('req', None, 'tp'), may hold values from -0.125 to 0.125
- up_weight: bfloat16 [16, 2048, 1408], P('req', None, 'tp'), may hold values from -0.125 to 0.125
- down_weight: bfloat16 [16, 1408, 2048], P('req', 'tp'), may hold values from -0.15625 to 0.15625
Outputs:
- attended: bfloat16 [2048, 2048], P('req', 'tp')
- mixed: bfloat16 [2048, 2048], P('req', 'tp')
Inputs may be any that keep to these rules, and one draw needn't show every extreme that they name: `page_table`: every row of a request is an order of its 12 pages. `prefix_len`: one request has a prefix of exactly 768. `routes`: in the rows of one request no expert is named more than 64 times, a bound that some block reaches.
All inputs are finite; a program needn't handle non-finite values.
Results may differ from a plain program's by a relative error of at most 0.023.
Values may be sent and summed in bfloat16 or wider, within the bound.
A program may use at most 64 MiB of HBM per device.

v0:
```python
import jax
import jax.numpy as jnp
from jax import lax
from jax.sharding import PartitionSpec as P

BLOCK_PAGES = 4


NEGATIVE = -1e30
EPSILON = 1e-06


def fold_keys(state, rows, keys, valid, rank, scale):
    maxima, totals, accum = state
    scores = (
        lax.dot_general(rows, keys, (((1,), (1,)), ((), ())), preferred_element_type=jnp.float32)
        * scale
    )
    masked = jnp.where(valid, scores, NEGATIVE)
    newtop = jnp.maximum(maxima, jnp.max(masked, axis=1))
    weights = jnp.where(valid, jnp.exp(masked - newtop[:, None]), 0.0)
    factor = jnp.exp(maxima - newtop)
    totals = totals * factor + jnp.sum(weights, axis=1)
    accum = accum * factor[:, None] + jnp.dot(
        weights.astype(jnp.bfloat16), keys[:, :rank], preferred_element_type=jnp.float32
    )
    return (newtop, totals, accum)


def merge_states(first, second):
    newtop = jnp.maximum(first[0], second[0])
    factor_one = jnp.exp(first[0] - newtop)
    factor_two = jnp.exp(second[0] - newtop)
    totals = first[1] * factor_one + second[1] * factor_two
    accum = first[2] * factor_one[:, None] + second[2] * factor_two[:, None]
    return (newtop, totals, accum)


def run_blocks(state, rows, keys_all, count_blocks, length, block, rank, scale):

    def step(index, carry):
        keys = lax.dynamic_slice_in_dim(keys_all, index * block, block, 0)
        valid = (index * block + jnp.arange(block, dtype=jnp.int32))[None, :] < length
        return fold_keys(carry, rows, keys, valid, rank, scale)

    return lax.fori_loop(0, count_blocks, step, state)


def on_device(
    queries,
    stretch_cache,
    prefix_pool,
    page_table,
    prefix_len,
    prompt_cache,
    prompt_len,
    group_ids,
    absorb_weight,
    value_weight,
    out_weight,
    residual,
    norm_gain,
    routes,
    route_weight,
    gate_weight,
    up_weight,
    down_weight,
):
    tokens, heads, width = queries.shape
    nope = absorb_weight.shape[1]
    rank = value_weight.shape[1]
    scale = width ** (-0.5)
    nope_part = jnp.einsum(
        "thn,hnr->thr", queries[:, :, :nope], absorb_weight, preferred_element_type=jnp.float32
    )
    absorbed = jnp.concatenate(
        [nope_part, queries[:, :, nope:].astype(jnp.float32)], axis=2
    ).astype(jnp.bfloat16)
    rows = absorbed.reshape(tokens * heads, width - nope + rank)
    count = rows.shape[0]
    empty = (
        jnp.full((count,), NEGATIVE, jnp.float32),
        jnp.zeros((count,), jnp.float32),
        jnp.zeros((count, rank), jnp.float32),
    )
    me_index = lax.axis_index("req")
    group = group_ids[me_index]
    prompt_length = prompt_len[group]
    own_length = prefix_len[me_index]
    causal = (
        jnp.arange(tokens, dtype=jnp.int32)[None, :]
        <= (jnp.arange(count, dtype=jnp.int32) // heads)[:, None]
    )
    stretch_state = fold_keys(empty, rows, stretch_cache, causal, rank, scale)
    keys = lax.dynamic_index_in_dim(
        lax.all_gather(prompt_cache, "req", axis=1, tiled=True), group, 0, keepdims=False
    )
    valid = jnp.arange(keys.shape[0], dtype=jnp.int32)[None, :] < prompt_length
    prompt_state = fold_keys(empty, rows, keys, valid, rank, scale)
    block = BLOCK_PAGES * prefix_pool.shape[1]
    prefix = jnp.take(prefix_pool, page_table[0], axis=0).reshape(-1, prefix_pool.shape[2])
    mine_blocks = (own_length + block - 1) // block
    prefix_state = run_blocks(empty, rows, prefix, mine_blocks, own_length, block, rank, scale)
    state = merge_states(merge_states(stretch_state, prompt_state), prefix_state)
    latent = (state[2] / state[1][:, None]).astype(jnp.bfloat16).reshape(tokens, heads, rank)
    heads_out = jnp.einsum(
        "thr,hrv->thv", latent, value_weight, preferred_element_type=jnp.float32
    ).astype(jnp.bfloat16)
    projected = jnp.dot(
        heads_out.reshape(tokens, -1), out_weight, preferred_element_type=jnp.float32
    )
    attention_part = lax.psum_scatter(
        projected.astype(jnp.bfloat16), "tp", scatter_dimension=1, tiled=True
    ).astype(jnp.float32)
    attended = (residual.astype(jnp.float32) + attention_part).astype(jnp.bfloat16)
    stream = attended.astype(jnp.float32)
    squares = lax.psum(jnp.sum(stream * stream, axis=1), "tp")
    model_width = out_weight.shape[1]
    normed = (
        stream * lax.rsqrt(squares / model_width + EPSILON)[:, None] * norm_gain.astype(jnp.float32)
    ).astype(jnp.bfloat16)
    experts = lax.axis_size("req")
    top = routes.shape[1]
    capacity = max(2, tokens * top * 4 // (3 * experts))
    flat = routes.reshape(-1)
    onehot = (flat[:, None] == jnp.arange(experts, dtype=jnp.int32)[None, :]).astype(jnp.int32)
    slot = jnp.sum(jnp.cumsum(onehot, axis=0) * onehot, axis=1) - 1
    dest = (flat * capacity + slot).reshape(tokens, top)
    places = jnp.arange(experts * capacity, dtype=jnp.int32)
    chooser = jnp.any(dest[None, :, :] == places[:, None, None], axis=2).astype(jnp.bfloat16)
    whole = lax.all_gather(normed, "tp", axis=1, tiled=True)
    buffer = (
        jnp.dot(chooser, whole, preferred_element_type=jnp.float32)
        .astype(jnp.bfloat16)
        .reshape(experts, capacity, -1)
    )
    received = lax.all_to_all(buffer, "req", split_axis=0, concat_axis=0, tiled=True)
    gate = jnp.einsum("snd,df->snf", received, gate_weight[0], preferred_element_type=jnp.float32)
    up = jnp.einsum("snd,df->snf", received, up_weight[0], preferred_element_type=jnp.float32)
    hidden = (jax.nn.silu(gate) * up).astype(jnp.bfloat16)
    part_out = jnp.einsum(
        "snf,fd->snd", hidden, down_weight[0], preferred_element_type=jnp.float32
    ).astype(jnp.bfloat16)
    returned = lax.all_to_all(part_out, "req", split_axis=0, concat_axis=0, tiled=True)
    flat_out = returned.reshape(experts * capacity, -1)
    combined = jnp.zeros((tokens, flat_out.shape[1]), jnp.float32)
    for choice_index in range(top):
        picked = jnp.take(flat_out, dest[:, choice_index], axis=0).astype(jnp.float32)
        combined = combined + route_weight[:, choice_index : choice_index + 1] * picked
    expert_part = lax.psum_scatter(
        combined.astype(jnp.bfloat16), "tp", scatter_dimension=1, tiled=True
    ).astype(jnp.float32)
    mixed = (stream + expert_part).astype(jnp.bfloat16)
    return (attended, mixed)


def solution(mesh):
    in_specs = (
        P("req", "tp", None),
        P("req", None),
        P("req", None, None),
        P("req", None),
        P(),
        P(None, "req", None),
        P(),
        P(),
        P("tp", None, None),
        P("tp", None, None),
        P("tp", None),
        P("req", "tp"),
        P("tp"),
        P("req", None),
        P("req", None),
        P("req", None, "tp"),
        P("req", None, "tp"),
        P("req", "tp", None),
    )
    out_specs = (P("req", "tp"), P("req", "tp"))
    return jax.shard_map(
        on_device, mesh=mesh, in_specs=in_specs, out_specs=out_specs, check_vma=False
    )
```

profile of v0, /device:TPU:8, one launch (start us, length us, event | category | flops | bytes accessed | tf_op | source)
XLA Modules:
  0.0 377.7 jit_solution(13195702632175572776)
XLA Ops:
  10.6 1.8 fusion.20
  12.4 1.6 copy.72
  14.2 2.5 pad_maximum_fusion
  17.4 1.8 fusion.39
  19.4 2.9 gather_fusion
  22.3 2.4 bitcast_select_fusion
  26.2 12.7 %while.14 = (s32[]{:T(128)}, f32[1024]{0:T(1024)S(1)}, f32[1024]{0:T(1024)S(1)}, f32[1024,512]{1,0:T(8,128)}, s32[]{:T(128)}, /*index=5*/s32[]{:T(128)}, bf16[76...) while((s32[]{:T(128)}, f32[1024]{0:T(1024)S(1)}, ...), condition=%wide.region_5.6_spmd, body=%wide.region_2.5_spmd.sunk | while | flops 573835776 | bytes 26084588 | solution.py:46
  27.1 2.1 fusion.81
  29.4 1.9 multiply_add_fusion.7
  33.4 2.1 fusion.81
  35.8 1.9 multiply_add_fusion.7
  42.8 27.1 %all_gather.6 = bf16[2,256,576]{2,1,0:T(8,128)(2,1)S(1)} all-gather(bf16[2,16,576]{2,1,0:T(8,128)(2,1)S(1)} %copy-done.12), channel_id=1, replica_groups=mesh['req'=16,'tp'=2] {'req'}, dimensions={1}, use_global_device_ids=true | all-gather | bytes 626688 | tf_op jit(solution)/shard_map/all_gather | solution.py:96
  69.9 2.0 fusion.61
  77.0 1.7 reduce-window.6
  79.8 11.6 %reduce-scatter.3.cloned.1.call-done = bf16[128,1024]{1,0:T(8,128)(2,1)} async-done(((bf16[128,2048]{1,0:T(8,128)(2,1)}), bf16[128,1024]{1,0:T(8,128)(2,1)}) %reduce-scatter.3.cloned.1.call-update) | async-done | bytes 262160 | tf_op jit(solution)/shard_map/reduce_scatter | solution.py:112
  92.5 4.9 %psum.7 = f32[128]{0:T(128)S(1)} all-reduce(f32[128]{0:T(128)S(1)} %get-tuple-element.81), channel_id=1, replica_groups=mesh['req'=16,'tp'=2] {'tp'}, use_global_device_ids=true, to_apply=%region_14.15 | all-reduce | flops 128 | bytes 1024 | tf_op jit(solution)/shard_map/psum | solution.py:117
  97.6 7.6 %all_gather.7 = bf16[128,2048]{1,0:T(8,128)(2,1)S(1)} all-gather(bf16[128,1024]{1,0:T(8,128)(2,1)S(1)} %fusion.31), channel_id=1, replica_groups=mesh['req'=16,'tp'=2] {'tp'}, dimensions={1}, use_global_device_ids=true | all-gather | bytes 786432 | tf_op jit(solution)/shard_map/all_gather | solution.py:131
  106.4 98.4 %all_to_all.10 = bf16[16,64,2048]{2,1,0:T(8,128)(2,1)S(1)} all-to-all(bf16[16,64,2048]{2,1,0:T(8,128)(2,1)S(1)} %bitcast.101), channel_id=1, replica_groups=mesh['req'=16,'tp'=2] {'req'}, dimensions={0} | all-to-all | bytes 8388608 | tf_op jit(solution)/shard_map/all_to_all | solution.py:137
  204.8 1.9 copy-done.5
  206.8 5.2 %fusion.14 = f32[16,64,704]{2,1,0:T(8,128)} fusion(bf16[16,64,2048]{2,1,0:T(8,128)(2,1)S(1)} %all_to_all.10, bf16[1,2048,704]{1,2,0:T(8,128)(2,1)S(1)} %copy-done.16), kind=kOutput, calls=%fused_computation.30 | convolution fusion | flops 2952790016 | bytes 9961472 | tf_op jit(solution)/shard_map/snd,df->snf/dot_general | solution.py:139
  212.0 12.3 %convolution_convert_fusion = bf16[16,64,2048]{2,1,0:T(8,128)(2,1)} fusion(bf16[1,704,2048]{2,1,0:T(8,128)(2,1)S(1)} %copy-done, f32[16,64,704]{2,1,0:T(8,128)} %fusion.14, bf16[16,64,2048]{2,1,0:T(8,128)(2,1)} %copy-done.5, bf16[1,2048,704]{1,2,0:T(8,128)(2,1)} %param.37), kind=kOutput, calls=%fused_computation.24 | convolution fusion | flops 5912002560 | bytes 17039360 | tf_op jit(solution)/shard_map/snf,fd->snd/dot_general | solution.py:141
  224.3 5.4 %all-to-all-start.1 = ((bf16[16,64,2048]{2,1,0:T(8,128)(2,1)}), bf16[16,64,2048]{2,1,0:T(8,128)(2,1)}, u32[]{:S(2)}, u32[]{:S(2)}) async-start(bf16[16,64,2048]{2,1,0:T(8,128)(2,1)} %convolution_convert_fusion), calls=%async_computation.2 | async-start | bytes 8388608 | tf_op jit(solution)/shard_map/all_to_all | solution.py:144
  229.8 90.7 %all-to-all-done.1 = bf16[16,64,2048]{2,1,0:T(8,128)(2,1)} async-done(((bf16[16,64,2048]{2,1,0:T(8,128)(2,1)}), bf16[16,64,2048]{2,1,0:T(8,128)(2,1)}, u32[]{:S(2)}, u32[]{:S(2)}) %all-to-all-start.1) | async-done | bytes 4194336 | tf_op jit(solution)/shard_map/all_to_all | solution.py:144
  320.5 5.0 %gather_fusion.4 = bf16[128,2048]{1,0:T(8,128)(2,1)} fusion(bf16[1024,2048]{1,0:T(8,128)(2,1)} %bitcast.24, s32[1024]{0:T(1024)S(1)} %get-tuple-element.117), kind=kCustom, calls=%fused_computation.3.clone | custom fusion | bytes 1049088 | tf_op jit(solution)/shard_map/jit(_take)/gather | solution.py:148
  325.5 5.0 %gather_fusion.1 = bf16[128,2048]{1,0:T(8,128)(2,1)} fusion(bf16[1024,2048]{1,0:T(8,128)(2,1)} %bitcast.24, s32[1024]{0:T(1024)S(1)} %get-tuple-element.120), kind=kCustom, calls=%fused_computation.clone | custom fusion | bytes 1049088 | tf_op jit(solution)/shard_map/jit(_take)/gather | solution.py:148
  330.5 5.0 %gather_fusion.2 = bf16[128,2048]{1,0:T(8,128)(2,1)} fusion(bf16[1024,2048]{1,0:T(8,128)(2,1)} %bitcast.24, s32[1024]{0:T(1024)S(1)} %get-tuple-element.119), kind=kCustom, calls=%fused_computation.1.clone | custom fusion | bytes 1049088 | tf_op jit(solution)/shard_map/jit(_take)/gather | solution.py:148
  335.4 5.0 %gather_fusion.3 = bf16[128,2048]{1,0:T(8,128)(2,1)} fusion(bf16[1024,2048]{1,0:T(8,128)(2,1)} %bitcast.24, s32[1024]{0:T(1024)S(1)} %get-tuple-element.118), kind=kCustom, calls=%fused_computation.2.clone | custom fusion | bytes 1049088 | tf_op jit(solution)/shard_map/jit(_take)/gather | solution.py:148
  340.4 5.0 %gather_fusion.5 = bf16[128,2048]{1,0:T(8,128)(2,1)} fusion(bf16[1024,2048]{1,0:T(8,128)(2,1)} %bitcast.24, s32[1024]{0:T(1024)S(1)} %get-tuple-element.116), kind=kCustom, calls=%fused_computation.4.clone | custom fusion | bytes 1049088 | tf_op jit(solution)/shard_map/jit(_take)/gather | solution.py:148
  345.4 5.0 %gather_fusion.6 = bf16[128,2048]{1,0:T(8,128)(2,1)} fusion(bf16[1024,2048]{1,0:T(8,128)(2,1)} %bitcast.24, s32[1024]{0:T(1024)S(1)} %get-tuple-element.115), kind=kCustom, calls=%fused_computation.5.clone | custom fusion | bytes 1049088 | tf_op jit(solution)/shard_map/jit(_take)/gather | solution.py:148
  350.4 3.6 add_convert_fusion
  354.0 15.2 %reduce-scatter.5.cloned.1.call-done = bf16[128,1024]{1,0:T(8,128)(2,1)} async-done(((bf16[128,2048]{1,0:T(8,128)(2,1)}), bf16[128,1024]{1,0:T(8,128)(2,1)}) %reduce-scatter.5.cloned.1.call-update) | async-done | bytes 262160 | tf_op jit(solution)/shard_map/reduce_scatter | solution.py:150
  369.2 1.7 fusion.32
  (103 shorter events, 20.6 us)
Async XLA Ops:
  7.2 204.8 %copy-start = (bf16[1,704,2048]{2,1,0:T(8,128)(2,1)S(1)}, bf16[1,704,2048]{2,1,0:T(8,128)(2,1)}, u32[]{:S(2)}) copy-start(bf16[1,704,2048]{2,1,0:T(8,128)(2,1)} %param.39) | copy-start | bytes 8650756
  7.2 6.8 %slice-start = ((bf16[128,8,192]{0,2,1:T(8,128)(2,1)}), bf16[128,8,64]{0,2,1:T(8,128)(2,1)S(1)}, s32[]{:S(2)}) async-start(bf16[128,8,192]{0,2,1:T(8,128)(2,1)} %param.22), calls=%async_computation.6 | async-start | bytes 262144 | tf_op jit(solution)/shard_map/slice | solution.py:77
  7.2 84.2 %reduce-scatter.3.cloned.1.call-start = ((), (), s32[]{:S(2)}) async-start(), calls=%async_computation.4 | async-start | bytes 786432 | tf_op jit(solution)/shard_map/reduce_scatter | solution.py:112
  12.4 4.3 %copy-start.11 = (bf16[128,576]{0,1:T(8,128)(2,1)S(1)}, bf16[128,576]{0,1:T(8,128)(2,1)}, u32[]{:S(2)}) copy-start(bf16[128,576]{0,1:T(8,128)(2,1)} %param.23) | copy-start | bytes 442372
  14.2 2.5 copy-start.6
  26.2 12.8 %copy-start.17 = (s32[16]{0:T(128)S(1)}, s32[16]{0:T(128)}, u32[]{:S(2)}) copy-start(s32[16]{0:T(128)} %param.29) | copy-start | bytes 196
  26.2 15.3 %copy-start.18 = (s32[2]{0:T(128)S(1)}, s32[2]{0:T(128)}, u32[]{:S(2)}) copy-start(s32[2]{0:T(128)} %param.28) | copy-start | bytes 28
  26.2 16.5 %copy-start.12 = (bf16[2,16,576]{2,1,0:T(8,128)(2,1)S(1)}, bf16[2,16,576]{2,1,0:T(8,128)(2,1)}, u32[]{:S(2)}) copy-start(bf16[2,16,576]{2,1,0:T(8,128)(2,1)} %param.27) | copy-start | bytes 110596
  26.3 3.1 copy-start.1
  31.3 1.3 copy-start.2
  32.6 3.1 copy-start.1
  37.7 1.3 copy-start.2
  69.9 2.3 copy-start.3
  69.9 2.5 copy-start.8
  72.4 1.3 copy-start.9
  72.4 2.5 copy-start.4
  75.0 1.6 copy-start.13
  75.0 2.0 copy-start.15
  75.0 16.4 %copy-start.10 = (bf16[128,1024]{1,0:T(8,128)(2,1)S(1)}, bf16[128,1024]{1,0:T(8,128)(2,1)}, u32[]{:S(2)}) copy-start(bf16[128,1024]{1,0:T(8,128)(2,1)} %param.33) | copy-start | bytes 786436
  92.5 276.7 %copy-start.7 = (bf16[128,1024]{1,0:T(8,128)(2,1)}, bf16[128,1024]{1,0:T(8,128)(2,1)S(1)}, u32[]{:S(2)}) copy-start(bf16[128,1024]{1,0:T(8,128)(2,1)S(1)} %get-tuple-element.82) | copy-start | bytes 786436
  106.4 100.4 %copy-start.16 = (bf16[1,2048,704]{1,2,0:T(8,128)(2,1)S(1)}, bf16[1,2048,704]{1,2,0:T(8,128)(2,1)}, u32[]{:S(2)}) copy-start(bf16[1,2048,704]{1,2,0:T(8,128)(2,1)} %param.38) | copy-start | bytes 8650756
  204.8 1.9 copy-start.5
  224.3 5.5 %copy-start.14 = (f32[128,6]{0,1:T(8,128)S(1)}, f32[128,6]{0,1:T(8,128)}, u32[]{:S(2)}) copy-start(f32[128,6]{0,1:T(8,128)} %param.36) | copy-start | bytes 9220
  224.3 96.2 %all-to-all-start.1 = ((bf16[16,64,2048]{2,1,0:T(8,128)(2,1)}), bf16[16,64,2048]{2,1,0:T(8,128)(2,1)}, u32[]{:S(2)}, u32[]{:S(2)}) async-start(bf16[16,64,2048]{2,1,0:T(8,128)(2,1)} %convolution_convert_fusion), calls=%async_computation.2 | async-start | bytes 8388608 | tf_op jit(solution)/shard_map/all_to_all | solution.py:144
  229.7 139.5 %reduce-scatter.5.cloned.1.call-start = ((), (), s32[]{:S(2)}) async-start(), calls=%async_computation.5 | async-start | bytes 786432 | tf_op jit(solution)/shard_map/reduce_scatter | solution.py:150
Sparse Core Ops, SparseCore 0:
  76.6 14.6 reduce-scatter.2
  354.1 15.0 reduce-scatter.4
where the time goes:
time: 380 us; the launch traced here: 378 us
  blocking collectives  138 us (36%)
  waiting for transfers between devices  117 us (31%)
  local copies, waits for them, and re-layouts  44.8 us (12%)
  matrix products  36.6 us (10%)
  other arithmetic  18.2 us (5%)
  between operations  17 us (4%)
  starting transfers between devices  5.47 us (1%)
    all_to_all x1, blocking collectives, on_device(): lax.all_to_all(buffer, 'req', split_axis=0, concat_axis=0, tiled=True)  98.4 us
    all_to_all x1, waiting for transfers between devices, on_device(): lax.all_to_all(part_out, 'req', split_axis=0, concat_axis=0, tiled=True)  90.7 us
    gather x6, local copies, waits for them, and re-layouts, on_device(): jnp.take(flat_out, dest[:, choice_index], axis=0).astype(jnp.float32)  29.9 us
    all_gather x1, blocking collectives, on_device(): lax.all_gather(prompt_cache, 'req', axis=1, tiled=True)  27.1 us
    reduce_scatter x1, waiting for transfers between devices, on_device(): lax.psum_scatter(combined.astype(jnp.bfloat16), 'tp', scatter_dimension=1...  15.2 us
    dot_general x1, matrix products, on_device(): jnp.einsum('snf,fd->snd', hidden, down_weight[0], preferred_element_type=...  12.3 us
    reduce_scatter x1, waiting for transfers between devices, on_device(): lax.psum_scatter(projected.astype(jnp.bfloat16), 'tp', scatter_dimension=...  11.6 us
  transfers between devices with their start and end apart: 3, of which 3 were waited for; matrix products, arithmetic and copies ran while one was open for 1% of the time, Pallas kernels for 0%

commit v1 on v0

--- a/solution.py
+++ b/solution.py
@@ -4,6 +4,7 @@
 from jax.sharding import PartitionSpec as P
 
 BLOCK_PAGES = 4
+GATHER_LIMIT = 4096
 
 
 NEGATIVE = -1e30
@@ -120,6 +121,20 @@
         stream * lax.rsqrt(squares / model_width + EPSILON)[:, None] * norm_gain.astype(jnp.float32)
     ).astype(jnp.bfloat16)
     experts = lax.axis_size("req")
+    if tokens * experts > GATHER_LIMIT:
+        return exchange_slots(
+            stream, normed, attended, routes, route_weight, gate_weight, up_weight, down_weight
+        )
+    return gather_tokens(
+        stream, normed, attended, routes, route_weight, gate_weight, up_weight, down_weight
+    )
+
+
+def exchange_slots(
+    stream, normed, attended, routes, route_weight, gate_weight, up_weight, down_weight
+):
+    tokens = routes.shape[0]
+    experts = lax.axis_size("req")
     top = routes.shape[1]
     capacity = max(2, tokens * top * 4 // (3 * experts))
     flat = routes.reshape(-1)
@@ -154,6 +169,41 @@
     return (attended, mixed)
 
 
+def gather_tokens(
+    stream, normed, attended, routes, route_weight, gate_weight, up_weight, down_weight
+):
+    tokens, top = routes.shape
+    experts = lax.axis_size("req")
+    capacity = max(2, tokens * top * 4 // (3 * experts))
+    choice = routes[:, :, None] == jnp.arange(experts, dtype=jnp.int32)[None, None, :]
+    share = jnp.sum(jnp.where(choice, route_weight[:, :, None], 0.0), axis=1)
+    mine = lax.all_to_all(share.T, "req", split_axis=0, concat_axis=0, tiled=True)
+    named = mine > 0.0
+    before = jnp.arange(tokens)[:, None] <= jnp.arange(tokens)[None, :]
+    slot = jnp.dot(
+        named.astype(jnp.bfloat16), before.astype(jnp.bfloat16), preferred_element_type=jnp.float32
+    ).astype(jnp.int32) - 1
+    chooser = (
+        (slot[:, None, :] == jnp.arange(capacity, dtype=jnp.int32)[None, :, None])
+        & named[:, None, :]
+    ).astype(jnp.bfloat16)
+    half = lax.all_gather(normed, "req", axis=0, tiled=True)
+    whole = lax.all_gather(half, "tp", axis=1, tiled=True).reshape(experts, tokens, -1)
+    rows = jnp.einsum("est,etd->esd", chooser, whole, preferred_element_type=jnp.float32)
+    rows = rows.astype(jnp.bfloat16).reshape(experts * capacity, -1)
+    gate = jnp.dot(rows, gate_weight[0], preferred_element_type=jnp.float32)
+    up = jnp.dot(rows, up_weight[0], preferred_element_type=jnp.float32)
+    hidden = (jax.nn.silu(gate) * up).astype(jnp.bfloat16)
+    part = jnp.dot(hidden, down_weight[0], preferred_element_type=jnp.float32)
+    part = part.astype(jnp.bfloat16).reshape(experts, capacity, -1)
+    spread = jnp.einsum("est,esd->etd", chooser, part, preferred_element_type=jnp.float32)
+    spread = (spread * mine[:, :, None]).astype(jnp.bfloat16).reshape(experts * tokens, -1)
+    summed = lax.psum_scatter(spread, "req", scatter_dimension=0, tiled=True)
+    expert_part = lax.psum_scatter(summed, "tp", scatter_dimension=1, tiled=True)
+    mixed = (stream + expert_part.astype(jnp.float32)).astype(jnp.bfloat16)
+    return (attended, mixed)
+
+
 def solution(mesh):
     in_specs = (
         P("req", "tp", None),

time: 380 us -> 414 us (1.089)
  waiting for transfers between devices: 117 us -> 282 us
  blocking collectives: 138 us -> 34.2 us
  local copies, waits for them, and re-layouts: 44.8 us -> 15.4 us
  matrix products: 36.6 us -> 50.6 us
  starting transfers between devices: 5.47 us -> 0.2 us
  other arithmetic: 18.2 us -> 14 us
    all_gather x0 -> x2, waiting for transfers between devices: none -> 146 us  [the longest x1 95.5 us: gather_tokens(): lax.all_gather(half, 'tp', axis=1, tiled=True).reshape(experts, tokens, -1)]
    reduce_scatter x1 -> x2, waiting for transfers between devices: 15.2 us -> 121 us  [the longest x1 105 us: gather_tokens(): summed = lax.psum_scatter(spread, 'req', scatter_dimension=0, tiled=True)]
    all_to_all x1 -> x0, waiting for transfers between devices: 90.7 us -> none  [on_device(): lax.all_to_all(part_out, 'req', split_axis=0, concat_axis=0, tiled=True)]
    all_to_all x1, blocking collectives: 98.4 us -> 8.43 us  [gather_tokens(): lax.all_to_all(share.T, 'req', split_axis=0, concat_axis=0, tiled=True)]
    gather x6 -> x0, local copies, waits for them, and re-layouts: 29.9 us -> none  [on_device(): jnp.take(flat_out, dest[:, choice_index], axis=0).astype(jnp.float32)]
    dot_general x3 -> x5, matrix products: 18.8 us -> 28.8 us  [the longest x1 11.3 us: gather_tokens(): part = jnp.dot(hidden, down_weight[0], preferred_element_type=jnp.float32)]
    all_gather x1 -> x0, blocking collectives: 7.55 us -> none  [on_device(): whole = lax.all_gather(normed, 'tp', axis=1, tiled=True)]
    all_gather x1, blocking collectives: 27.1 us -> 20.7 us  [on_device(): lax.all_gather(prompt_cache, 'req', axis=1, tiled=True)]
  transfers between devices with their start and end apart: 3 -> 5, of which waited for: 3 -> 5; matrix products, arithmetic and copies ran while one was open for 1% -> 0% of each run, Pallas kernels for 0% -> 0%
where the time goes in v1:
time: 414 us
  waiting for transfers between devices  282 us (68%)
  matrix products  50.6 us (12%)
  blocking collectives  34.2 us (8%)
  between operations  16.6 us (4%)
  local copies, waits for them, and re-layouts  15.4 us (4%)
  other arithmetic  14 us (3%)
    reduce_scatter x1, waiting for transfers between devices, gather_tokens(): summed = lax.psum_scatter(spread, 'req', scatter_dimension=0, tiled=True)  105 us
    all_gather x1, waiting for transfers between devices, gather_tokens(): lax.all_gather(half, 'tp', axis=1, tiled=True).reshape(experts, tokens, -1)  95.5 us
    all_gather x1, waiting for transfers between devices, gather_tokens(): half = lax.all_gather(normed, 'req', axis=0, tiled=True)  50.8 us
    all_gather x1, blocking collectives, on_device(): lax.all_gather(prompt_cache, 'req', axis=1, tiled=True)  20.7 us
    reduce_scatter x1, waiting for transfers between devices, gather_tokens(): lax.psum_scatter(summed, 'tp', scatter_dimension=1, tiled=True)  16.3 us
    reduce_scatter x1, waiting for transfers between devices, on_device(): lax.psum_scatter(projected.astype(jnp.bfloat16), 'tp', scatter_dimension=...  14.7 us
    dot_general x1, matrix products, gather_tokens(): part = jnp.dot(hidden, down_weight[0], preferred_element_type=jnp.float32)  11.3 us
    dot_general x5, matrix products, fold_keys(): jnp.dot(weights.astype(jnp.bfloat16), keys[:, :rank], preferred_element_t...  8.82 us
  transfers between devices with their start and end apart: 5, of which 5 were waited for; matrix products, arithmetic and copies ran while one was open for 0% of the time, Pallas kernels for 0%

profile of v1, /device:TPU:8, one launch (start us, length us, event | category | flops | bytes accessed | tf_op | source)
XLA Modules:
  0.0 413.6 jit_solution(9794841471749217400)
XLA Ops:
  7.2 1.4 dynamic_slice.19
  10.6 1.8 fusion.19
  12.4 1.6 copy.60
  14.2 2.5 pad_maximum_fusion
  17.4 1.8 fusion.42
  19.4 2.9 gather_fusion
  22.3 2.4 bitcast_select_fusion
  24.6 1.6 broadcast_in_dim.113
  26.2 19.1 %while.14 = (s32[]{:T(128)}, f32[1024]{0:T(1024)S(1)}, f32[1024]{0:T(1024)S(1)}, f32[1024,512]{1,0:T(8,128)}, s32[]{:T(128)}, /*index=5*/s32[]{:T(128)}, bf16[76...) while((s32[]{:T(128)}, f32[1024]{0:T(1024)S(1)}, ...), condition=%wide.region_5.6_spmd, body=%wide.region_2.5_spmd.sunk | while | flops 573835776 | bytes 26084588 | solution.py:47
  27.1 2.1 fusion.88
  29.4 1.9 multiply_add_fusion.6
  31.3 1.3 copy-done.2
  33.4 2.1 fusion.88
  35.8 1.9 multiply_add_fusion.6
  39.8 2.1 fusion.88
  42.1 1.9 multiply_add_fusion.6
  49.2 20.7 %all_gather.9 = bf16[2,256,576]{2,1,0:T(8,128)(2,1)S(1)} all-gather(bf16[2,16,576]{2,1,0:T(8,128)(2,1)S(1)} %copy-done.12), channel_id=1, replica_groups=mesh['req'=16,'tp'=2] {'req'}, dimensions={1}, use_global_device_ids=true | all-gather | bytes 626688 | tf_op jit(solution)/shard_map/all_gather | solution.py:97
  69.9 2.0 fusion.68
  75.0 1.5 convolution_convert_fusion.2
  76.6 14.7 %reduce-scatter.4.cloned.1.call-done = bf16[128,1024]{1,0:T(8,128)(2,1)} async-done(((bf16[128,2048]{1,0:T(8,128)(2,1)}), bf16[128,1024]{1,0:T(8,128)(2,1)}) %reduce-scatter.4.cloned.1.call-update) | async-done | bytes 262160 | tf_op jit(solution)/shard_map/reduce_scatter | solution.py:113
  92.4 5.1 %psum.7 = f32[128]{0:T(128)S(1)} all-reduce(f32[128]{0:T(128)S(1)} %get-tuple-element.68), channel_id=1, replica_groups=mesh['req'=16,'tp'=2] {'tp'}, use_global_device_ids=true, to_apply=%region_11.12 | all-reduce | flops 128 | bytes 1024 | tf_op jit(solution)/shard_map/psum | solution.py:118
  98.4 50.8 %all-gather.3.cloned.1.call-done = bf16[2048,1024]{1,0:T(8,128)(2,1)} async-done(((bf16[128,1024]{1,0:T(8,128)(2,1)}), bf16[2048,1024]{1,0:T(8,128)(2,1)}) %all-gather.3.cloned.1.call-update) | async-done | bytes 4194320 | tf_op jit(solution)/shard_map/all_gather | solution.py:190
  149.3 8.4 %all_to_all.12 = f32[16,1,128]{2,1,0:T(1,128)S(1)} all-to-all(f32[16,1,128]{2,1,0:T(1,128)S(1)} %bitcast.78), channel_id=1, replica_groups=mesh['req'=16,'tp'=2] {'req'}, dimensions={0} | all-to-all | bytes 16384 | tf_op jit(solution)/shard_map/all_to_all | solution.py:180
  157.9 95.5 %all-gather.5.cloned.1.call-done = bf16[2048,2048]{1,0:T(8,128)(2,1)} async-done(((bf16[2048,1024]{1,0:T(8,128)(2,1)}), bf16[2048,2048]{1,0:T(8,128)(2,1)}) %all-gather.5.cloned.1.call-update) | async-done | bytes 8388624 | tf_op jit(solution)/shard_map/all_gather | solution.py:191
  253.4 4.8 %convolution_convert_fusion.1 = bf16[16,64,2048]{2,1,0:T(8,128)(2,1)S(1)} fusion(bf16[16,128,2048]{2,1,0:T(8,128)(2,1)} %bitcast.64, s32[16,128]{1,0:T(8,128)S(1)} %fusion.23, pred[16,128]{1,0:T(8,128)(4,1)S(1)} %compare_bitcast_fusion), kind=kOutput, calls=%fused_computation.20 | convolution fusion | flops 539230208 | bytes 12593152 | tf_op jit(solution)/shard_map/est,etd->esd/dot_general | solution.py:192
  258.2 1.9 copy-done.4
  260.1 4.8 %fusion.13 = f32[1024,704]{0,1:T(8,128)} fusion(bf16[1024,2048]{1,0:T(8,128)(2,1)S(1)} %bitcast.65, bf16[1,2048,704]{1,2,0:T(8,128)(2,1)S(1)} %copy-done.16), kind=kOutput, calls=%fused_computation.22 | convolution fusion | flops 2952790016 | bytes 9961472 | tf_op jit(solution)/shard_map/dot_general | solution.py:195
  264.9 11.3 %convolution_convert_fusion = bf16[1024,2048]{1,0:T(8,128)(2,1)} fusion(bf16[1,704,2048]{2,1,0:T(8,128)(2,1)S(1)} %copy-done, f32[1024,704]{0,1:T(8,128)} %fusion.13, bf16[1024,2048]{1,0:T(8,128)(2,1)} %bitcast.66, bf16[1,2048,704]{1,2,0:T(8,128)(2,1)} %param.35), kind=kOutput, calls=%fused_computation.19 | convolution fusion | flops 5912002560 | bytes 17039360 | tf_op jit(solution)/shard_map/dot_general | solution.py:197
  276.2 7.8 %multiply_convert_fusion = bf16[16,128,2048]{2,1,0:T(8,128)(2,1)} fusion(f32[16,128]{1,0:T(8,128)S(1)} %bitcast.77, bf16[16,64,2048]{2,1,0:T(8,128)(2,1)} %bitcast.70, s32[16,128]{1,0:T(8,128)S(1)} %fusion.23, pred[16,128]{1,0:T(8,128)(4,1)S(1)} %compare_bitcast_fusion), kind=kOutput, calls=%fused_computation.18 | convolution fusion | flops 545521664 | bytes 12601344 | tf_op jit(solution)/shard_map/est,esd->etd/dot_general | solution.py:199
  284.1 104.9 %reduce-scatter.6.cloned.1.call-done = bf16[128,2048]{1,0:T(8,128)(2,1)} async-done(((bf16[2048,2048]{1,0:T(8,128)(2,1)}), bf16[128,2048]{1,0:T(8,128)(2,1)}) %reduce-scatter.6.cloned.1.call-update) | async-done | bytes 524304 | tf_op jit(solution)/shard_map/reduce_scatter | solution.py:201
  389.1 16.3 %reduce-scatter.8.cloned.1.call-done = bf16[128,1024]{1,0:T(8,128)(2,1)} async-done(((bf16[128,2048]{1,0:T(8,128)(2,1)}), bf16[128,1024]{1,0:T(8,128)(2,1)}) %reduce-scatter.8.cloned.1.call-update) | async-done | bytes 262160 | tf_op jit(solution)/shard_map/reduce_scatter | solution.py:202
  405.4 1.7 fusion.32
  (99 shorter events, 15.4 us)
Async XLA Ops:
  7.2 257.7 %copy-start = (bf16[1,704,2048]{2,1,0:T(8,128)(2,1)S(1)}, bf16[1,704,2048]{2,1,0:T(8,128)(2,1)}, u32[]{:S(2)}) copy-start(bf16[1,704,2048]{2,1,0:T(8,128)(2,1)} %param.37) | copy-start | bytes 8650756
  7.2 6.8 %slice-start = ((bf16[128,8,192]{0,2,1:T(8,128)(2,1)}), bf16[128,8,64]{0,2,1:T(8,128)(2,1)S(1)}, s32[]{:S(2)}) async-start(bf16[128,8,192]{0,2,1:T(8,128)(2,1)} %param.20), calls=%async_computation.9 | async-start | bytes 262144 | tf_op jit(solution)/shard_map/slice | solution.py:78
  7.2 84.1 %reduce-scatter.4.cloned.1.call-start = ((), (), s32[]{:S(2)}) async-start(), calls=%async_computation.4 | async-start | bytes 786432 | tf_op jit(solution)/shard_map/reduce_scatter | solution.py:113
  12.4 4.3 %copy-start.11 = (bf16[128,576]{0,1:T(8,128)(2,1)S(1)}, bf16[128,576]{0,1:T(8,128)(2,1)}, u32[]{:S(2)}) copy-start(bf16[128,576]{0,1:T(8,128)(2,1)} %param.21) | copy-start | bytes 442372
  14.2 2.5 copy-start.6
  26.2 19.1 %copy-start.17 = (s32[16]{0:T(128)S(1)}, s32[16]{0:T(128)}, u32[]{:S(2)}) copy-start(s32[16]{0:T(128)} %param.27) | copy-start | bytes 196
  26.2 21.7 %copy-start.18 = (s32[2]{0:T(128)S(1)}, s32[2]{0:T(128)}, u32[]{:S(2)}) copy-start(s32[2]{0:T(128)} %param.26) | copy-start | bytes 28
  26.2 22.9 %copy-start.12 = (bf16[2,16,576]{2,1,0:T(8,128)(2,1)S(1)}, bf16[2,16,576]{2,1,0:T(8,128)(2,1)}, u32[]{:S(2)}) copy-start(bf16[2,16,576]{2,1,0:T(8,128)(2,1)} %param.25) | copy-start | bytes 110596
  26.3 3.1 copy-start.1
  31.3 1.3 copy-start.2
  32.6 3.1 copy-start.1
  37.7 1.3 copy-start.2
  39.0 3.1 copy-start.1
  44.0 1.3 copy-start.2
  69.9 2.3 copy-start.3
  69.9 2.5 copy-start.8
  72.4 1.3 copy-start.9
  72.4 2.5 copy-start.5
  74.9 1.6 copy-start.15
  74.9 16.3 %copy-start.10 = (bf16[128,1024]{1,0:T(8,128)(2,1)S(1)}, bf16[128,1024]{1,0:T(8,128)(2,1)}, u32[]{:S(2)}) copy-start(bf16[128,1024]{1,0:T(8,128)(2,1)} %param.31) | copy-start | bytes 786436
  76.5 72.7 %all-gather.3.cloned.1.call-start = ((), (), s32[]{:S(2)}) async-start(), calls=%async_computation.5 | async-start | bytes 4456448 | tf_op jit(solution)/shard_map/all_gather | solution.py:190
  92.4 313.0 %copy-start.7 = (bf16[128,1024]{1,0:T(8,128)(2,1)}, bf16[128,1024]{1,0:T(8,128)(2,1)S(1)}, u32[]{:S(2)}) copy-start(bf16[128,1024]{1,0:T(8,128)(2,1)S(1)} %get-tuple-element.69) | copy-start | bytes 786436
  92.4 56.9 %copy-start.13 = (f32[128,6]{0,1:T(8,128)S(1)}, f32[128,6]{0,1:T(8,128)}, u32[]{:S(2)}) copy-start(f32[128,6]{0,1:T(8,128)} %param.34) | copy-start | bytes 9220
  92.4 56.9 %copy-start.14 = (s32[128,6]{0,1:T(8,128)S(1)}, s32[128,6]{0,1:T(8,128)}, u32[]{:S(2)}) copy-start(s32[128,6]{0,1:T(8,128)} %param.33) | copy-start | bytes 9220
  98.4 155.0 %all-gather.5.cloned.1.call-start = ((), (), s32[]{:S(2)}) async-start(), calls=%async_computation.6 | async-start | bytes 12582912 | tf_op jit(solution)/shard_map/all_gather | solution.py:191
  149.3 239.8 %reduce-scatter.6.cloned.1.call-start = ((), (), s32[]{:S(2)}) async-start(), calls=%async_computation.7 | async-start | bytes 8912896 | tf_op jit(solution)/shard_map/reduce_scatter | solution.py:201
  253.4 6.7 %copy-start.16 = (bf16[1,2048,704]{1,2,0:T(8,128)(2,1)S(1)}, bf16[1,2048,704]{1,2,0:T(8,128)(2,1)}, u32[]{:S(2)}) copy-start(bf16[1,2048,704]{1,2,0:T(8,128)(2,1)} %param.36) | copy-start | bytes 8650756
  258.2 1.9 copy-start.4
  284.1 121.3 %reduce-scatter.8.cloned.1.call-start = ((), (), s32[]{:S(2)}) async-start(), calls=%async_computation.8 | async-start | bytes 786432 | tf_op jit(solution)/shard_map/reduce_scatter | solution.py:202
Sparse Core Ops, SparseCore 0:
  76.6 14.5 reduce-scatter.3
  98.5 50.7 all-gather.2
  150.9 102.4 all-gather.4
  284.2 104.8 reduce-scatter.5
  391.2 14.0 reduce-scatter.7

commit v2 on v0

--- a/solution.py
+++ b/solution.py
@@ -1,6 +1,8 @@
 import jax
 import jax.numpy as jnp
 from jax import lax
+from jax.experimental import pallas as pl
+from jax.experimental.pallas import tpu as pltpu
 from jax.sharding import PartitionSpec as P
 
 BLOCK_PAGES = 4
@@ -119,6 +121,15 @@
     normed = (
         stream * lax.rsqrt(squares / model_width + EPSILON)[:, None] * norm_gain.astype(jnp.float32)
     ).astype(jnp.bfloat16)
+    return exchange_slots(
+        stream, normed, attended, routes, route_weight, gate_weight, up_weight, down_weight
+    )
+
+
+def exchange_slots(
+    stream, normed, attended, routes, route_weight, gate_weight, up_weight, down_weight
+):
+    tokens = routes.shape[0]
     experts = lax.axis_size("req")
     top = routes.shape[1]
     capacity = max(2, tokens * top * 4 // (3 * experts))
@@ -152,6 +163,523 @@
     ).astype(jnp.float32)
     mixed = (stream + expert_part).astype(jnp.bfloat16)
     return (attended, mixed)
+
+
+MESH = pl.DeviceIdType.MESH
+
+
+def coordinates():
+    me = lax.axis_index("req")
+    return me // 4, (me // 2) % 2, me % 2, lax.axis_index("tp")
+
+
+def place(z, x, core, y):
+    return {"req": (z * 2 + x) * 2 + core, "tp": y}
+
+
+def prompt_kernel(block_ref, share_ref, keys_ref, mine_ref, send, recv, send_w, recv_w, local):
+    me = lax.axis_index("req")
+    y = lax.axis_index("tp")
+    barrier = pltpu.get_barrier_semaphore()
+    for step in range(1, 16):
+        pl.semaphore_signal(
+            barrier, inc=1, device_id={"req": (me + step) % 16, "tp": y}, device_id_type=MESH
+        )
+    pl.semaphore_wait(barrier, 15)
+    rows = pl.ds(pl.multiple_of(me * 16, 16), 16)
+
+    def copies(step):
+        peer = (me + step) % 16
+        block = pltpu.make_async_remote_copy(
+            block_ref, keys_ref.at[:, rows, :], send.at[step], recv.at[step],
+            device_id={"req": peer, "tp": y}, device_id_type=MESH,
+        )
+        share = pltpu.make_async_remote_copy(
+            share_ref.at[peer], mine_ref.at[me], send_w.at[step], recv_w.at[step],
+            device_id={"req": peer, "tp": y}, device_id_type=MESH,
+        )
+        return block, share
+
+    for step in range(1, 16):
+        block, share = copies(step)
+        block.start()
+        share.start()
+    own = pltpu.make_async_copy(block_ref, keys_ref.at[:, rows, :], local.at[0])
+    own_share = pltpu.make_async_copy(share_ref.at[me], mine_ref.at[me], local.at[1])
+    own.start()
+    own_share.start()
+    own.wait()
+    own_share.wait()
+    for step in range(1, 16):
+        block, share = copies(step)
+        block.wait()
+        share.wait()
+
+
+def share_prompts(prompt_cache, share):
+    groups, rows, width = prompt_cache.shape
+    tokens = share.shape[2]
+    return pl.pallas_call(
+        prompt_kernel,
+        out_shape=(
+            jax.ShapeDtypeStruct((groups, rows * 16, width), prompt_cache.dtype),
+            jax.ShapeDtypeStruct((16, 1, tokens), jnp.float32),
+        ),
+        in_specs=[pl.BlockSpec(memory_space=pltpu.VMEM)] * 2,
+        out_specs=(pl.BlockSpec(memory_space=pltpu.VMEM),) * 2,
+        scratch_shapes=[pltpu.SemaphoreType.DMA((16,))] * 4 + [pltpu.SemaphoreType.DMA((2,))],
+        compiler_params=pltpu.CompilerParams(collective_id=0, has_side_effects=True),
+    )(prompt_cache, share)
+
+
+def greet():
+    z, x, core, y = coordinates()
+    barrier = pltpu.get_barrier_semaphore()
+    for peer in (place(z, 1 - x, core, y), place(z, x, core, 1 - y), place(z, x, 1 - core, y)):
+        pl.semaphore_signal(barrier, inc=1, device_id=peer, device_id_type=MESH)
+
+    @pl.when(z < 3)
+    def _():
+        pl.semaphore_signal(barrier, inc=1, device_id=place(z + 1, x, core, y), device_id_type=MESH)
+
+    @pl.when(z > 0)
+    def _():
+        pl.semaphore_signal(barrier, inc=1, device_id=place(z - 1, x, core, y), device_id_type=MESH)
+
+    pl.semaphore_wait(barrier, 3 + (1 - z // 3) + (z + 2) // 3)
+
+
+def spread_tokens(whole, send, recv):
+    z, x, core, y = coordinates()
+    half_rows, half_cols = whole.shape[1] // 2, whole.shape[2] // 2
+
+    def piece(zp, xp, yp, half, cp):
+        return whole.at[
+            (zp * 2 + xp) * 2 + cp,
+            pl.ds(half * half_rows, half_rows),
+            pl.ds(pl.multiple_of(yp * half_cols, half_cols), half_cols),
+        ]
+
+    def hop(zp, xp, yp, half, cp, kind, peer):
+        slot = zp * 8 + xp * 4 + yp * 2 + half
+        part = piece(zp, xp, yp, half, cp)
+        return pltpu.make_async_remote_copy(
+            part, part, send.at[kind, slot], recv.at[cp, slot], device_id=peer, device_id_type=MESH
+        )
+
+    up, down = place(z + 1, x, core, y), place(z - 1, x, core, y)
+    over_x, over_y, other = place(z, 1 - x, core, y), place(z, x, core, 1 - y), place(z, x, 1 - core, y)
+
+    def column(zp, finish):
+        for half in range(2):
+            for go, kind, peer in (
+                ((zp <= z) & (z < 3), 0, up), ((zp >= z) & (z > 0), 1, down)
+            ):
+                @pl.when(go)
+                def _(kind=kind, peer=peer):
+                    copy = hop(zp, x, y, half, core, kind, peer)
+                    copy.wait_send() if finish else copy.start()
+        for kind, peer, half in ((2, over_x, 0), (3, over_y, 1), (2, over_x, 1), (3, over_y, 0)):
+            copy = hop(zp, x, y, half, core, kind, peer)
+            copy.wait_send() if finish else copy.start()
+        for half in range(2):
+            copy = hop(zp, x, y, half, core, 4, other)
+            copy.wait_send() if finish else copy.start()
+
+    def beside(zp, finish):
+        if not finish:
+            for half in range(2):
+                hop(zp, 1 - x, y, half, core, 2, over_x).wait_recv()
+                hop(zp, x, 1 - y, half, core, 3, over_y).wait_recv()
+        copies = [hop(zp, 1 - x, y, 0, core, 3, over_y), hop(zp, x, 1 - y, 1, core, 2, over_x)]
+        for half in range(2):
+            copies.append(hop(zp, 1 - x, y, half, core, 4, other))
+            copies.append(hop(zp, x, 1 - y, half, core, 4, other))
+        for copy in copies:
+            copy.wait_send() if finish else copy.start()
+
+    def diagonal(zp, finish):
+        for half in range(2):
+            copy = hop(zp, 1 - x, 1 - y, half, core, 4, other)
+            if finish:
+                copy.wait_send()
+            else:
+                hop(zp, 1 - x, 1 - y, half, core, 2, over_x).wait_recv()
+                copy.start()
+
+    def each(distance, work):
+        if distance == 0:
+            work(z)
+            return
+
+        @pl.when(z + distance < 4)
+        def _():
+            work(z + distance)
+
+        @pl.when(z - distance >= 0)
+        def _():
+            work(z - distance)
+
+    def arrive(zp):
+        for half in range(2):
+            hop(zp, x, y, half, core, 0, over_x).wait_recv()
+        column(zp, False)
+
+    column(z, False)
+    for distance in range(1, 4):
+        each(distance, arrive)
+        each(distance - 1, lambda zp: beside(zp, False))
+        if distance > 1:
+            each(distance - 2, lambda zp: diagonal(zp, False))
+    each(3, lambda zp: beside(zp, False))
+    each(2, lambda zp: diagonal(zp, False))
+    each(3, lambda zp: diagonal(zp, False))
+
+    def close(zp, carry):
+        for xp in range(2):
+            for yp in range(2):
+                for half in range(2):
+                    hop(zp, xp, yp, half, 1 - core, 4, other).wait_recv()
+        column(zp, True)
+        beside(zp, True)
+        diagonal(zp, True)
+        return carry
+
+    lax.fori_loop(0, 4, close, 0)
+
+
+def return_sums(compute, acc, core_in, x_diag, y_diag, x_in, y_in, up_in, down_in, sems):
+    z, x, core, y = coordinates()
+    rows, half_cols = acc.shape[2], acc.shape[3] // 2
+    half_rows = rows // 2
+    up, down = place(z + 1, x, core, y), place(z - 1, x, core, y)
+    over_x, over_y, other = place(z, 1 - x, core, y), place(z, x, core, 1 - y), place(z, x, 1 - core, y)
+    mine = pl.ds(pl.multiple_of(y * half_cols, half_cols), half_cols)
+    theirs = pl.ds(pl.multiple_of((1 - y) * half_cols, half_cols), half_cols)
+    top, low = pl.ds(0, half_rows), pl.ds(half_rows, half_rows)
+
+    def copy(source, target, kind, zp, peer):
+        return pltpu.make_async_remote_copy(
+            source, target, sems.at[0, kind, zp], sems.at[1, kind, zp],
+            device_id=peer, device_id_type=MESH,
+        )
+
+    def block(zp, xp, cp):
+        return acc.at[zp, xp * 2 + cp]
+
+    def core_copy(zp, xp):
+        return copy(block(zp, xp, 1 - core), core_in.at[zp, xp], xp, zp, other)
+
+    def diag_copies(zp):
+        far = block(zp, 1 - x, core)
+        return (
+            copy(far.at[top, theirs], y_diag.at[zp], 2, zp, over_y),
+            copy(far.at[low, theirs], x_diag.at[zp], 3, zp, over_x),
+        )
+
+    def free_copies(zp):
+        return (
+            copy(block(zp, 1 - x, core).at[low, mine], x_in.at[zp, low], 4, zp, over_x),
+            copy(block(zp, x, core).at[top, theirs], y_in.at[zp, top], 5, zp, over_y),
+        )
+
+    def last_copies(zp):
+        return (
+            copy(block(zp, 1 - x, core).at[top, mine], x_in.at[zp, top], 6, zp, over_x),
+            copy(block(zp, x, core).at[low, theirs], y_in.at[zp, low], 7, zp, over_y),
+        )
+
+    def up_copy(zp):
+        return copy(block(zp, x, core).at[:, mine], up_in.at[zp], 8, zp, up)
+
+    def down_copy(zp):
+        return copy(block(zp, x, core).at[:, mine], down_in.at[zp], 9, zp, down)
+
+    def add(target, *terms):
+        total = target[...].astype(jnp.float32)
+        for term in terms:
+            total = total + term[...].astype(jnp.float32)
+        target[...] = total.astype(target.dtype)
+
+    def cores(zp):
+        for xp in range(2):
+            core_copy(zp, xp).wait_recv()
+            add(block(zp, xp, core), core_in.at[zp, xp])
+        for item in diag_copies(zp) + free_copies(zp):
+            item.start()
+
+    def corners(zp):
+        from_y, from_x = diag_copies(zp)
+        over_x_copy, over_y_copy = last_copies(zp)
+        from_y.wait_recv()
+        add(block(zp, 1 - x, core).at[top, mine], y_diag.at[zp])
+        over_x_copy.start()
+        from_x.wait_recv()
+        add(block(zp, x, core).at[low, theirs], x_diag.at[zp])
+        over_y_copy.start()
+
+    def columns(zp):
+        for item in free_copies(zp) + last_copies(zp):
+            item.wait_recv()
+        own = block(zp, x, core).at[:, mine]
+        add(own, x_in.at[zp], y_in.at[zp])
+
+        @pl.when((z > 0) & (zp >= z))
+        def _():
+            up_copy(zp).wait_recv()
+            add(own, up_in.at[zp])
+
+        @pl.when((z < 3) & (zp <= z))
+        def _():
+            down_copy(zp).wait_recv()
+            add(own, down_in.at[zp])
+
+        @pl.when(zp > z)
+        def _():
+            up_copy(zp).start()
+
+        @pl.when(zp < z)
+        def _():
+            down_copy(zp).start()
+
+    def turn(step):
+        return (3 - step // 2) * (1 - step % 2) + (step // 2) * (step % 2)
+
+    def stage(step, carry):
+        @pl.when(step < 4)
+        def _():
+            zp = turn(step)
+            compute(zp)
+            for xp in range(2):
+                core_copy(zp, xp).start()
+
+        @pl.when((step >= 1) & (step < 5))
+        def _():
+            cores(turn(step - 1))
+
+        @pl.when((step >= 2) & (step < 6))
+        def _():
+            corners(turn(step - 2))
+
+        @pl.when(step >= 3)
+        def _():
+            columns(turn(step - 3))
+
+        return carry
+
+    lax.fori_loop(0, 7, stage, 0)
+
+    def close(zp, carry):
+        for xp in range(2):
+            core_copy(zp, xp).wait_send()
+        for item in diag_copies(zp) + free_copies(zp) + last_copies(zp):
+            item.wait_send()
+
+        @pl.when(zp > z)
+        def _():
+            up_copy(zp).wait_send()
+
+        @pl.when(zp < z)
+        def _():
+            down_copy(zp).wait_send()
+
+        return carry
+
+    lax.fori_loop(0, 4, close, 0)
+    return block(z, x, core).at[:, mine]
+
+
+def expert_kernel(
+    projected, residual, gain, chooser, slot_weight, gate_hbm, up_hbm, down_hbm,
+    attended, mixed,
+    whole, outgoing, incoming, squares_out, squares_in, gate_w, up_w, down_w, rows, hidden,
+    acc, core_in, x_diag, y_diag, x_in, y_in, up_in, down_in,
+    pair_sems, load_sems, send, recv, sems,
+):
+    z, x, core, y = coordinates()
+    half_cols = residual.shape[1]
+    loads = [
+        pltpu.make_async_copy(source, target, load_sems.at[index])
+        for index, (source, target) in enumerate(
+            ((gate_hbm, gate_w), (up_hbm, up_w), (down_hbm, down_w))
+        )
+    ]
+    for load in loads:
+        load.start()
+    mine = pl.ds(pl.multiple_of(y * half_cols, half_cols), half_cols)
+    theirs = pl.ds(pl.multiple_of((1 - y) * half_cols, half_cols), half_cols)
+    over_y = place(z, x, core, 1 - y)
+    outgoing[...] = projected[:, theirs].astype(jnp.bfloat16)
+    greet()
+    swap = pltpu.make_async_remote_copy(
+        outgoing, incoming, pair_sems.at[0], pair_sems.at[1], device_id=over_y, device_id_type=MESH
+    )
+    swap.start()
+    swap.wait()
+    stream = residual[...].astype(jnp.float32) + projected[:, mine] + incoming[...].astype(jnp.float32)
+    attended[...] = stream.astype(jnp.bfloat16)
+    stream = attended[...].astype(jnp.float32)
+    sums = jnp.sum(stream * stream, axis=1, keepdims=True)
+    squares_out[...] = jnp.broadcast_to(sums, squares_out.shape)
+    pair = pltpu.make_async_remote_copy(
+        squares_out, squares_in, pair_sems.at[2], pair_sems.at[3],
+        device_id=over_y, device_id_type=MESH,
+    )
+    pair.start()
+    pair.wait()
+    both = sums + squares_in[:, :1]
+    scaled = stream * lax.rsqrt(both / (2 * half_cols) + EPSILON) * gain[...].astype(jnp.float32)
+    whole[(z * 2 + x) * 2 + core, :, mine] = scaled.astype(jnp.bfloat16)
+    spread_tokens(whole, send, recv)
+    for load in loads:
+        load.wait()
+    capacity = chooser.shape[1]
+
+    def compute(zp):
+        for index in range(4):
+            picked = jnp.dot(
+                chooser[zp * 4 + index], whole[zp * 4 + index], preferred_element_type=jnp.float32
+            )
+            rows[pl.ds(index * capacity, capacity), :] = picked.astype(jnp.bfloat16)
+        gate = jnp.dot(rows[...], gate_w[...], preferred_element_type=jnp.float32)
+        up = jnp.dot(rows[...], up_w[...], preferred_element_type=jnp.float32)
+        level = slot_weight[pl.ds(pl.multiple_of(zp * 4 * capacity, 4 * capacity), 4 * capacity), :]
+        hidden[...] = (gate / (1.0 + jnp.exp(-gate)) * up * level).astype(jnp.bfloat16)
+        part = jnp.dot(hidden[...], down_w[...], preferred_element_type=jnp.float32)
+        part = part.astype(jnp.bfloat16)
+        for index in range(4):
+            acc[zp, index] = lax.dot_general(
+                chooser[zp * 4 + index], part[index * capacity : (index + 1) * capacity],
+                (((0,), (0,)), ((), ())), preferred_element_type=jnp.float32,
+            ).astype(jnp.bfloat16)
+
+    own = return_sums(compute, acc, core_in, x_diag, y_diag, x_in, y_in, up_in, down_in, sems)
+    mixed[...] = (attended[...].astype(jnp.float32) + own[...].astype(jnp.float32)).astype(jnp.bfloat16)
+
+
+def run_experts(projected, residual, gain, chooser, slot_weight, gate_w, up_w, down_w):
+    tokens, width = projected.shape
+    half = residual.shape[1]
+    capacity = chooser.shape[1]
+    units = gate_w.shape[1]
+    bf16, f32 = jnp.bfloat16, jnp.float32
+    dma = pltpu.SemaphoreType.DMA
+    vmem = pl.BlockSpec(memory_space=pltpu.VMEM)
+    anywhere = pl.BlockSpec(memory_space=pl.ANY)
+    return pl.pallas_call(
+        expert_kernel,
+        out_shape=(jax.ShapeDtypeStruct((tokens, half), bf16),) * 2,
+        in_specs=[vmem] * 5 + [anywhere] * 3,
+        out_specs=(vmem, vmem),
+        scratch_shapes=[
+            pltpu.VMEM((16, tokens, width), bf16),
+            pltpu.VMEM((tokens, half), bf16),
+            pltpu.VMEM((tokens, half), bf16),
+            pltpu.VMEM((tokens, 128), f32),
+            pltpu.VMEM((tokens, 128), f32),
+            pltpu.VMEM((width, units), bf16),
+            pltpu.VMEM((width, units), bf16),
+            pltpu.VMEM((units, width), bf16),
+            pltpu.VMEM((4 * capacity, width), bf16),
+            pltpu.VMEM((4 * capacity, units), bf16),
+            pltpu.VMEM((4, 4, tokens, width), bf16),
+            pltpu.VMEM((4, 2, tokens, width), bf16),
+            pltpu.VMEM((4, tokens // 2, half), bf16),
+            pltpu.VMEM((4, tokens // 2, half), bf16),
+            pltpu.VMEM((4, tokens, half), bf16),
+            pltpu.VMEM((4, tokens, half), bf16),
+            pltpu.VMEM((4, tokens, half), bf16),
+            pltpu.VMEM((4, tokens, half), bf16),
+            dma((4,)),
+            dma((3,)),
+            dma((5, 32)),
+            dma((2, 32)),
+            dma((2, 10, 4)),
+        ],
+        compiler_params=pltpu.CompilerParams(
+            collective_id=1, has_side_effects=True, vmem_limit_bytes=58 << 20
+        ),
+    )(projected, residual, gain, chooser, slot_weight, gate_w, up_w, down_w)
+
+
+def on_block(
+    queries, stretch_cache, prefix_pool, page_table, prefix_len, prompt_cache, prompt_len,
+    group_ids, absorb_weight, value_weight, out_weight, residual, norm_gain, routes,
+    route_weight, gate_weight, up_weight, down_weight,
+):
+    tokens, heads, width = queries.shape
+    nope, rank = absorb_weight.shape[1], value_weight.shape[1]
+    experts, top = lax.axis_size("req"), routes.shape[1]
+    capacity = max(2, tokens * top * 4 // (3 * experts))
+    me = lax.axis_index("req")
+    choice = routes[:, :, None] == jnp.arange(experts, dtype=jnp.int32)[None, None, :]
+    share = jnp.sum(jnp.where(choice, route_weight[:, :, None], 0.0), axis=1)
+    prompts, mine = share_prompts(prompt_cache, share.T[:, None, :])
+    mine = mine[:, 0, :]
+    named = mine > 0.0
+    before = jnp.arange(tokens)[:, None] <= jnp.arange(tokens)[None, :]
+    slot = jnp.dot(
+        named.astype(jnp.bfloat16), before.astype(jnp.bfloat16), preferred_element_type=jnp.float32
+    ).astype(jnp.int32) - 1
+    picks = (
+        slot[:, None, :] == jnp.arange(capacity, dtype=jnp.int32)[None, :, None]
+    ) & named[:, None, :]
+    chooser = picks.astype(jnp.bfloat16)
+    slot_weight = jnp.sum(jnp.where(picks, mine[:, None, :], 0.0), axis=2).reshape(-1, 1)
+
+    group = group_ids[me]
+    pages, page = prefix_pool.shape[:2]
+    order = jnp.arange(pages, dtype=jnp.int32)
+    logical = jnp.sum(
+        jnp.where(page_table[0][None, :] == order[:, None], order[None, :], 0), axis=1
+    )
+    prefix_at = (logical[:, None] * page + jnp.arange(page, dtype=jnp.int32)[None, :]).reshape(-1)
+    prompt = lax.dynamic_index_in_dim(prompts, group, 0, keepdims=False)
+    keys = jnp.concatenate(
+        [stretch_cache, prompt, prefix_pool.reshape(pages * page, -1)], axis=0
+    )
+    seen = jnp.concatenate(
+        [jnp.arange(prompt.shape[0]) < prompt_len[group], prefix_at < prefix_len[me]]
+    )
+    token = jnp.arange(tokens)
+    visible = jnp.concatenate(
+        [
+            token[None, :] <= token[:, None],
+            jnp.broadcast_to(seen[None, :], (tokens, seen.shape[0])),
+        ],
+        axis=1,
+    )
+    turned = jnp.transpose(queries, (1, 0, 2))
+    absorbed = jnp.concatenate(
+        [
+            jnp.einsum(
+                "htn,hnr->htr", turned[:, :, :nope], absorb_weight,
+                preferred_element_type=jnp.float32,
+            ).astype(jnp.bfloat16),
+            turned[:, :, nope:],
+        ],
+        axis=2,
+    )
+    scores = jnp.einsum("htc,kc->htk", absorbed, keys, preferred_element_type=jnp.float32)
+    scores = jnp.where(visible[None], scores * width ** (-0.5), NEGATIVE)
+    weights = jnp.exp(scores - jnp.max(scores, axis=2, keepdims=True))
+    weights = jnp.where(visible[None], weights, 0.0)
+    totals = jnp.sum(weights, axis=2, keepdims=True)
+    latent = jnp.einsum(
+        "htk,kr->htr", weights.astype(jnp.bfloat16), keys[:, :rank],
+        preferred_element_type=jnp.float32,
+    )
+    latent = (latent / totals).astype(jnp.bfloat16)
+    heads_out = jnp.einsum(
+        "htr,hrv->thv", latent, value_weight, preferred_element_type=jnp.float32
+    ).astype(jnp.bfloat16)
+    projected = jnp.dot(
+        heads_out.reshape(tokens, -1), out_weight, preferred_element_type=jnp.float32
+    )
+    return run_experts(
+        projected, residual, norm_gain[None, :], chooser, slot_weight,
+        gate_weight[0], up_weight[0], down_weight[0],
+    )
 
 
 def solution(mesh):
@@ -176,6 +704,7 @@
         P("req", "tp", None),
     )
     out_specs = (P("req", "tp"), P("req", "tp"))
+    body = on_block if mesh.shape["req"] == 16 and mesh.shape["tp"] == 2 else on_device
     return jax.shard_map(
-        on_device, mesh=mesh, in_specs=in_specs, out_specs=out_specs, check_vma=False
-    )
+        body, mesh=mesh, in_specs=in_specs, out_specs=out_specs, check_vma=False
+    )

time: 380 us -> 204 us (0.54)
  Pallas kernels: 0 us -> 154 us
  blocking collectives: 138 us -> 0 us
  waiting for transfers between devices: 117 us -> 0 us
  local copies, waits for them, and re-layouts: 44.8 us -> 23 us
  matrix products: 36.6 us -> 15.6 us
  between operations: 17 us -> 2.69 us
  other arithmetic: 18.2 us -> 7.65 us
  starting transfers between devices: 5.47 us -> 0 us
    pallas_call x0 -> x2, Pallas kernels: none -> 154 us  [the longest x1 133 us: run_experts(): pl.pallas_call(expert_kernel, out_shape=(jax.ShapeDtypeStruct((tokens, ha...]
    all_to_all x1 -> x0, blocking collectives: 98.4 us -> none  [on_device(): lax.all_to_all(buffer, 'req', split_axis=0, concat_axis=0, tiled=True)]
    all_to_all x1 -> x0, waiting for transfers between devices: 90.7 us -> none  [on_device(): lax.all_to_all(part_out, 'req', split_axis=0, concat_axis=0, tiled=True)]
    all_gather x2 -> x0, blocking collectives: 34.6 us -> none  [the longest x1 27.1 us: on_device(): lax.all_gather(prompt_cache, 'req', axis=1, tiled=True)]
    gather x7 -> x0, local copies, waits for them, and re-layouts: 32.7 us -> none  [the longest x6 29.9 us: on_device(): jnp.take(flat_out, dest[:, choice_index], axis=0).astype(jnp.float32)]
    dot_general x14 -> x4, matrix products: 36.6 us -> 8.98 us  [the longest x1 3.94 us: on_block(): jnp.dot(heads_out.reshape(tokens, -1), out_weight, preferred_element_type...]
    reduce_scatter x2 -> x0, waiting for transfers between devices: 26.8 us -> none  [the longest x1 15.2 us: on_device(): lax.psum_scatter(combined.astype(jnp.bfloat16), 'tp', scatter_dimension=1...]
    unnamed x35 -> x8, local copies, waits for them, and re-layouts: 2.66 us -> 13.8 us
  transfers between devices with their start and end apart: 3 -> 0, of which waited for: 3 -> 0; matrix products, arithmetic and copies ran while one was open for 1% -> 0% of each run, Pallas kernels for 0% -> 0%
where the time goes in v2:
time: 204 us; the launch traced here: 203 us
  Pallas kernels  154 us (75%)
  local copies, waits for them, and re-layouts  23 us (11%)
  matrix products  15.6 us (8%)
  other arithmetic  7.65 us (4%)
  between operations  2.69 us (1%)
    pallas_call x1, Pallas kernels, run_experts(): pl.pallas_call(expert_kernel, out_shape=(jax.ShapeDtypeStruct((tokens, ha...  133 us
    pallas_call x1, Pallas kernels, share_prompts(): pl.pallas_call(prompt_kernel, out_shape=(jax.ShapeDtypeStruct((groups, ro...  20.6 us
    unnamed x8, local copies, waits for them, and re-layouts  13.8 us
    sub x1, matrix products, on_block(): weights = jnp.exp(scores - jnp.max(scores, axis=2, keepdims=True))  6.65 us

profile of v2, /device:TPU:8, one launch (start us, length us, event | category | flops | bytes accessed | tf_op | source)
XLA Modules:
  0.0 202.7 jit_solution(10434045252684137611)
XLA Ops:
  0.6 0.0 copy-start
  0.6 1.3 dynamic_slice.13
  3.9 1.2 dynamic_slice.14
  5.2 0.6 iota_compare_fusion.6
  5.8 1.2 dynamic_slice.15
  7.1 0.8 select_reduce_fusion.2
  7.8 0.7 add_compare_fusion
  8.6 0.1 lt.30
  8.7 1.3 broadcast_in_dim.93.gain
  9.9 1.3 select_reduce_fusion.1
  11.3 0.7 pad_add_fusion
  12.0 1.2 copy.34
  13.2 0.0 copy-done
  13.3 0.4 convolution_convert_fusion
  13.7 20.6 %shard_map.185 = (bf16[2,256,576]{2,1,0:T(8,128)(2,1)}, f32[16,1,128]{2,1,0:T(1,128)}) custom-call(bf16[2,16,576]{2,1,0:T(8,128)(2,1)} %block_ref.1, f32[16,1,128]{2,1,0:T(1,128)} %bitcast.45), custom_call_target="tpu_custom_call" | custom-call | tf_op jit(solution)/shard_map/pallas_call | solution.py:222
  34.3 1.0 constant_dynamic-slice_fusion
  35.3 0.2 copy.35
  35.4 0.8 fusion.17
  36.3 0.7 broadcast_compare_fusion
  37.0 0.9 select_reduce_fusion
  37.9 0.8 fusion.20.chooser
  38.7 1.3 reshape.35.slot_weight
  40.0 1.5 copy.36
  41.5 6.6 %fusion.26 = (f32[8,128]{1,0:T(8,128)}, bf16[8,128,1152]{2,1,0:T(8,128)(2,1)}) fusion(pred[128,1152]{1,0:T(8,128)(4,1)} %pad_add_fusion, bf16[8,128,64]{2,1,0:T(8,128)(2,1)S(1)} %slice.13, bf16[8,128,512]{2,1,0:T(8,128)(2,1)S(1)} %convolution_convert_fusion, bf16[768,576]{0,1:T(8,128)(2,1)S(1)} %copy.36, bf16[256,576]{0,1:T(8,128)(2,1)S(1)} %bitcast.39, ...), kind=kOutput, calls=%fused_computation.43 | convolution fusion | flops 1372374144 | bytes 5017600 | tf_op jit(solution)/shard_map/sub | solution.py:665
  48.1 1.0 pad_maximum_fusion
  49.2 3.8 %fusion.14 = bf16[8,128,128]{1,2,0:T(8,128)(2,1)S(1)} fusion(bf16[8,512,128]{2,1,0:T(8,128)(2,1)} %param.27, bf16[8,128,1152]{2,1,0:T(8,128)(2,1)} %get-tuple-element.7, bf16[1152,576]{0,1:T(8,128)(2,1)S(1)} %pad_maximum_fusion, f32[8,128]{1,0:T(8,128)} %get-tuple-element.6), kind=kOutput, calls=%fused_computation.15 | convolution fusion | flops 1343356928 | bytes 4853760 | tf_op jit(solution)/shard_map/htr,hrv->thv/dot_general | solution.py:673
  53.0 3.9 %fusion.31.projected = f32[128,2048]{1,0:T(8,128)} fusion(bf16[128,1024]{0,1:T(8,128)(2,1)S(1)} %bitcast.42, bf16[1024,2048]{1,0:T(8,128)(2,1)} %param.28), kind=kOutput, calls=%fused_computation.44 | convolution fusion | flops 536870912 | bytes 5505024 | tf_op jit(solution)/shard_map/dot_general | solution.py:676
  56.9 4.6 %copy.40 = bf16[1,2048,704]{2,1,0:T(8,128)(2,1)} copy(bf16[1,2048,704]{1,2,0:T(8,128)(2,1)} %param.33) | data formatting | bytes 5767168 | tf_op args[15]
  61.5 4.6 %copy.41 = bf16[1,2048,704]{2,1,0:T(8,128)(2,1)} copy(bf16[1,2048,704]{1,2,0:T(8,128)(2,1)} %param.34) | data formatting | bytes 5767168 | tf_op args[16]
  66.2 133.2 %shard_map.186 = (bf16[128,1024]{1,0:T(8,128)(2,1)}, bf16[128,1024]{1,0:T(8,128)(2,1)}) custom-call(f32[128,2048]{1,0:T(8,128)} %fusion.31.projected, bf16[128,1024]{1,0:T(8,128)(2,1)} %residual.1, bf16[1,1024]{1,0:T(2,128)(2,1)} %broadcast_in_dim.93.gain, bf16[16,64,128]{2,1,0:T(8,128)(2,1)} %fusion.20.chooser, f32[1024,1]{1,0:T(8,128)} %reshape.35.slot_weight, ...), custom_call_target="tpu_custom_call" | custom-call | tf_op jit(solution)/shard_map/pallas_call | solution.py:569
  199.4 1.7 copy.52
  201.1 1.7 copy.53
  (6 shorter events, 0.1 us)
Async XLA Ops:
  0.6 12.6 %copy-start = (bf16[8,128,512]{2,1,0:T(8,128)(2,1)S(1)}, bf16[8,128,512]{2,1,0:T(8,128)(2,1)}, u32[]{:S(2)}) copy-start(bf16[8,128,512]{2,1,0:T(8,128)(2,1)} %param.26) | copy-start | bytes 3145732

commit v3 on v2

--- a/solution.py
+++ b/solution.py
@@ -188,32 +188,69 @@
     pl.semaphore_wait(barrier, 15)
     rows = pl.ds(pl.multiple_of(me * 16, 16), 16)
 
-    def copies(step):
+    def shares(step):
         peer = (me + step) % 16
-        block = pltpu.make_async_remote_copy(
-            block_ref, keys_ref.at[:, rows, :], send.at[step], recv.at[step],
-            device_id={"req": peer, "tp": y}, device_id_type=MESH,
-        )
-        share = pltpu.make_async_remote_copy(
+        return pltpu.make_async_remote_copy(
             share_ref.at[peer], mine_ref.at[me], send_w.at[step], recv_w.at[step],
             device_id={"req": peer, "tp": y}, device_id_type=MESH,
         )
-        return block, share
-
+
+    core, other = me % 2, me + 1 - 2 * (me % 2)
+
+    def relay(step):
+        source = (me + 2 * step) % 16
+        lines = pl.ds(pl.multiple_of(source * 16, 16), 16)
+        arrival = pltpu.make_async_remote_copy(
+            keys_ref.at[:, lines, :], keys_ref.at[:, lines, :], send.at[8 - step],
+            recv.at[8 - step], device_id={"req": source, "tp": y}, device_id_type=MESH,
+        )
+        passing = pltpu.make_async_remote_copy(
+            keys_ref.at[:, lines, :], keys_ref.at[:, lines, :], send.at[8 + source // 2],
+            recv.at[8 + source // 2], device_id={"req": other, "tp": y}, device_id_type=MESH,
+        )
+        return arrival, passing
+
+    def arriving(step):
+        source = (me + 2 * step) % 16 + 1 - 2 * core
+        lines = pl.ds(pl.multiple_of(source * 16, 16), 16)
+        return pltpu.make_async_remote_copy(
+            keys_ref.at[:, lines, :], keys_ref.at[:, lines, :], send.at[8 + source // 2],
+            recv.at[8 + source // 2], device_id={"req": other, "tp": y}, device_id_type=MESH,
+        )
+
+    def direct(step):
+        return pltpu.make_async_remote_copy(
+            block_ref, keys_ref.at[:, rows, :], send.at[step], recv.at[step],
+            device_id={"req": (me + 2 * step) % 16, "tp": y}, device_id_type=MESH,
+        )
+
+    home = pltpu.make_async_remote_copy(
+        block_ref, keys_ref.at[:, rows, :], send.at[8 + me // 2], recv.at[8 + me // 2],
+        device_id={"req": other, "tp": y}, device_id_type=MESH,
+    )
+    for step in range(1, 8):
+        direct(step).start()
+    home.start()
     for step in range(1, 16):
-        block, share = copies(step)
-        block.start()
-        share.start()
+        shares(step).start()
     own = pltpu.make_async_copy(block_ref, keys_ref.at[:, rows, :], local.at[0])
     own_share = pltpu.make_async_copy(share_ref.at[me], mine_ref.at[me], local.at[1])
     own.start()
     own_share.start()
     own.wait()
     own_share.wait()
+    for step in range(1, 8):
+        arrival, passing = relay(step)
+        arrival.wait_recv()
+        passing.start()
+    for step in range(8):
+        arriving(step).wait_recv()
+    home.wait_send()
+    for step in range(1, 8):
+        direct(step).wait_send()
+        relay(step)[1].wait_send()
     for step in range(1, 16):
-        block, share = copies(step)
-        block.wait()
-        share.wait()
+        shares(step).wait()
 
 
 def share_prompts(prompt_cache, share):
@@ -249,7 +286,7 @@
     pl.semaphore_wait(barrier, 3 + (1 - z // 3) + (z + 2) // 3)
 
 
-def spread_tokens(whole, send, recv):
+def spread_tokens(whole, send, recv, finish):
     z, x, core, y = coordinates()
     half_rows, half_cols = whole.shape[1] // 2, whole.shape[2] // 2
 
@@ -307,39 +344,38 @@
                 hop(zp, 1 - x, 1 - y, half, core, 2, over_x).wait_recv()
                 copy.start()
 
-    def each(distance, work):
-        if distance == 0:
-            work(z)
-            return
-
-        @pl.when(z + distance < 4)
-        def _():
-            work(z + distance)
-
-        @pl.when(z - distance >= 0)
-        def _():
-            work(z - distance)
-
     def arrive(zp):
         for half in range(2):
             hop(zp, x, y, half, core, 0, over_x).wait_recv()
         column(zp, False)
 
-    column(z, False)
-    for distance in range(1, 4):
-        each(distance, arrive)
-        each(distance - 1, lambda zp: beside(zp, False))
-        if distance > 1:
-            each(distance - 2, lambda zp: diagonal(zp, False))
-    each(3, lambda zp: beside(zp, False))
-    each(2, lambda zp: diagonal(zp, False))
-    each(3, lambda zp: diagonal(zp, False))
-
-    def close(zp, carry):
+    def ready(zp):
         for xp in range(2):
             for yp in range(2):
                 for half in range(2):
                     hop(zp, xp, yp, half, 1 - core, 4, other).wait_recv()
+        finish(zp)
+
+    column(z, False)
+
+    def turn(step, carry):
+        for lag, work, first in (
+            (0, arrive, 1), (2, lambda zp: beside(zp, False), 0),
+            (4, lambda zp: diagonal(zp, False), 0), (5, ready, 0),
+        ):
+            item = step - lag
+            distance = (item + 1) // 2
+            zp = z + distance * (2 * (item % 2) - 1)
+
+            @pl.when((item >= first) & (item < 7) & (zp >= 0) & (zp < 4))
+            def _(work=work, zp=zp):
+                work(zp)
+
+        return carry
+
+    lax.fori_loop(1, 12, turn, 0)
+
+    def close(zp, carry):
         column(zp, True)
         beside(zp, True)
         diagonal(zp, True)
@@ -348,7 +384,15 @@
     lax.fori_loop(0, 4, close, 0)
 
 
-def return_sums(compute, acc, core_in, x_diag, y_diag, x_in, y_in, up_in, down_in, sems):
+def core_hop(acc, core_in, sems, zp, xp):
+    z, x, core, y = coordinates()
+    return pltpu.make_async_remote_copy(
+        acc.at[zp, xp * 2 + 1 - core], core_in.at[zp, xp], sems.at[0, xp, zp], sems.at[1, xp, zp],
+        device_id=place(z, x, 1 - core, y), device_id_type=MESH,
+    )
+
+
+def return_sums(acc, core_in, x_diag, y_diag, x_in, y_in, up_in, down_in, sems):
     z, x, core, y = coordinates()
     rows, half_cols = acc.shape[2], acc.shape[3] // 2
     half_rows = rows // 2
@@ -368,7 +412,7 @@
         return acc.at[zp, xp * 2 + cp]
 
     def core_copy(zp, xp):
-        return copy(block(zp, xp, 1 - core), core_in.at[zp, xp], xp, zp, other)
+        return core_hop(acc, core_in, sems, zp, xp)
 
     def diag_copies(zp):
         far = block(zp, 1 - x, core)
@@ -448,26 +492,19 @@
     def stage(step, carry):
         @pl.when(step < 4)
         def _():
-            zp = turn(step)
-            compute(zp)
-            for xp in range(2):
-                core_copy(zp, xp).start()
+            cores(turn(step))
 
         @pl.when((step >= 1) & (step < 5))
         def _():
-            cores(turn(step - 1))
-
-        @pl.when((step >= 2) & (step < 6))
-        def _():
-            corners(turn(step - 2))
-
-        @pl.when(step >= 3)
-        def _():
-            columns(turn(step - 3))
+            corners(turn(step - 1))
+
+        @pl.when(step >= 2)
+        def _():
+            columns(turn(step - 2))
 
         return carry
 
-    lax.fori_loop(0, 7, stage, 0)
+    lax.fori_loop(0, 6, stage, 0)
 
     def close(zp, carry):
         for xp in range(2):
@@ -530,7 +567,6 @@
     both = sums + squares_in[:, :1]
     scaled = stream * lax.rsqrt(both / (2 * half_cols) + EPSILON) * gain[...].astype(jnp.float32)
     whole[(z * 2 + x) * 2 + core, :, mine] = scaled.astype(jnp.bfloat16)
-    spread_tokens(whole, send, recv)
     for load in loads:
         load.wait()
     capacity = chooser.shape[1]
@@ -541,8 +577,9 @@
                 chooser[zp * 4 + index], whole[zp * 4 + index], preferred_element_type=jnp.float32
             )
             rows[pl.ds(index * capacity, capacity), :] = picked.astype(jnp.bfloat16)
-        gate = jnp.dot(rows[...], gate_w[...], preferred_element_type=jnp.float32)
-        up = jnp.dot(rows[...], up_w[...], preferred_element_type=jnp.float32)
+        across = (((1,), (1,)), ((), ()))
+        gate = lax.dot_general(rows[...], gate_w[...], across, preferred_element_type=jnp.float32)
+        up = lax.dot_general(rows[...], up_w[...], across, preferred_element_type=jnp.float32)
         level = slot_weight[pl.ds(pl.multiple_of(zp * 4 * capacity, 4 * capacity), 4 * capacity), :]
         hidden[...] = (gate / (1.0 + jnp.exp(-gate)) * up * level).astype(jnp.bfloat16)
         part = jnp.dot(hidden[...], down_w[...], preferred_element_type=jnp.float32)
@@ -553,7 +590,11 @@
                 (((0,), (0,)), ((), ())), preferred_element_type=jnp.float32,
             ).astype(jnp.bfloat16)
 
-    own = return_sums(compute, acc, core_in, x_diag, y_diag, x_in, y_in, up_in, down_in, sems)
+        for xp in range(2):
+            core_hop(acc, core_in, sems, zp, xp).start()
+
+    spread_tokens(whole, send, recv, compute)
+    own = return_sums(acc, core_in, x_diag, y_diag, x_in, y_in, up_in, down_in, sems)
     mixed[...] = (attended[...].astype(jnp.float32) + own[...].astype(jnp.float32)).astype(jnp.bfloat16)
 
 
@@ -561,7 +602,7 @@
     tokens, width = projected.shape
     half = residual.shape[1]
     capacity = chooser.shape[1]
-    units = gate_w.shape[1]
+    units = gate_w.shape[0]
     bf16, f32 = jnp.bfloat16, jnp.float32
     dma = pltpu.SemaphoreType.DMA
     vmem = pl.BlockSpec(memory_space=pltpu.VMEM)
@@ -577,8 +618,8 @@
             pltpu.VMEM((tokens, half), bf16),
             pltpu.VMEM((tokens, 128), f32),
             pltpu.VMEM((tokens, 128), f32),
-            pltpu.VMEM((width, units), bf16),
-            pltpu.VMEM((width, units), bf16),
+            pltpu.VMEM((units, width), bf16),
+            pltpu.VMEM((units, width), bf16),
             pltpu.VMEM((units, width), bf16),
             pltpu.VMEM((4 * capacity, width), bf16),
             pltpu.VMEM((4 * capacity, units), bf16),
@@ -627,19 +668,22 @@
     chooser = picks.astype(jnp.bfloat16)
     slot_weight = jnp.sum(jnp.where(picks, mine[:, None, :], 0.0), axis=2).reshape(-1, 1)
 
-    group = group_ids[me]
+    requests = jnp.arange(group_ids.shape[0], dtype=jnp.int32) == me
+    group = jnp.sum(jnp.where(requests, group_ids, 0))
+    own_length = jnp.sum(jnp.where(requests, prefix_len, 0))
+    prompt_length = jnp.where(group == 0, prompt_len[0], prompt_len[1])
     pages, page = prefix_pool.shape[:2]
     order = jnp.arange(pages, dtype=jnp.int32)
     logical = jnp.sum(
         jnp.where(page_table[0][None, :] == order[:, None], order[None, :], 0), axis=1
     )
     prefix_at = (logical[:, None] * page + jnp.arange(page, dtype=jnp.int32)[None, :]).reshape(-1)
-    prompt = lax.dynamic_index_in_dim(prompts, group, 0, keepdims=False)
+    prompt = jnp.where(group == 0, prompts[0], prompts[1])
     keys = jnp.concatenate(
         [stretch_cache, prompt, prefix_pool.reshape(pages * page, -1)], axis=0
     )
     seen = jnp.concatenate(
-        [jnp.arange(prompt.shape[0]) < prompt_len[group], prefix_at < prefix_len[me]]
+        [jnp.arange(prompt.shape[0]) < prompt_length, prefix_at < own_length]
     )
     token = jnp.arange(tokens)
     visible = jnp.concatenate(
@@ -678,7 +722,7 @@
     )
     return run_experts(
         projected, residual, norm_gain[None, :], chooser, slot_weight,
-        gate_weight[0], up_weight[0], down_weight[0],
+        jnp.swapaxes(gate_weight[0], 0, 1), jnp.swapaxes(up_weight[0], 0, 1), down_weight[0],
     )
 
 

time: 204 us -> 194 us (0.951)
  local copies, waits for them, and re-layouts: 23 us -> 9.65 us
    unnamed x8 -> x12, local copies, waits for them, and re-layouts: 13.8 us -> 4.61 us
    pallas_call x1, Pallas kernels: 133 us -> 142 us  [run_experts(): pl.pallas_call(expert_kernel, out_shape=(jax.ShapeDtypeStruct((tokens, ha...]
    pallas_call x1, Pallas kernels: 20.6 us -> 14.9 us  [share_prompts(): pl.pallas_call(prompt_kernel, out_shape=(jax.ShapeDtypeStruct((groups, ro...]
    dynamic_slice x5 -> x0, local copies, waits for them, and re-layouts: 4.98 us -> none  [the longest x1 1.33 us: on_block(): group = group_ids[me]]
where the time goes in v3:
time: 194 us; the launch traced here: 192 us
  Pallas kernels  156 us (80%)
  matrix products  16.1 us (8%)
  local copies, waits for them, and re-layouts  9.65 us (5%)
  other arithmetic  7.48 us (4%)
  between operations  2.78 us (1%)
    pallas_call x1, Pallas kernels, run_experts(): pl.pallas_call(expert_kernel, out_shape=(jax.ShapeDtypeStruct((tokens, ha...  142 us
    pallas_call x1, Pallas kernels, share_prompts(): pl.pallas_call(prompt_kernel, out_shape=(jax.ShapeDtypeStruct((groups, ro...  14.9 us
    sub x1, matrix products, on_block(): weights = jnp.exp(scores - jnp.max(scores, axis=2, keepdims=True))  6.82 us
    unnamed x12, local copies, waits for them, and re-layouts  4.61 us
    dot_general x1, matrix products, on_block(): jnp.dot(heads_out.reshape(tokens, -1), out_weight, preferred_element_type...  3.94 us

profile of v3, /device:TPU:8, one launch (start us, length us, event | category | flops | bytes accessed | tf_op | source)
XLA Modules:
  0.0 192.4 jit_solution(10616837627768284042)
XLA Ops:
  0.6 0.0 copy-start
  0.6 1.4 fusion.24
  2.7 1.3 fusion.28
  5.4 0.8 select_reduce_fusion.2
  6.2 0.7 add_compare_fusion
  6.9 0.1 lt.19
  7.1 1.3 select_reduce_fusion.1
  8.4 14.9 %shard_map.185 = (bf16[2,256,576]{2,1,0:T(8,128)(2,1)}, f32[16,1,128]{2,1,0:T(1,128)}) custom-call(bf16[2,16,576]{2,1,0:T(8,128)(2,1)} %block_ref.1, f32[16,1,128]{2,1,0:T(1,128)} %bitcast.47), custom_call_target="tpu_custom_call" | custom-call | tf_op jit(solution)/shard_map/pallas_call | solution.py:259
  23.2 1.1 select_bitcast_fusion
  24.4 0.2 copy.32
  24.5 0.0 copy-start.1
  24.5 1.2 copy.31
  25.8 0.0 copy-done
  25.8 1.4 convolution_convert_fusion
  27.2 1.5 copy.33
  28.8 0.0 copy-done.1
  28.8 6.8 %fusion.29 = (f32[8,128]{1,0:T(8,128)}, bf16[8,128,1152]{2,1,0:T(8,128)(2,1)}) fusion(pred[128,1152]{1,0:T(8,128)(4,1)S(1)} %pad_add_fusion, bf16[8,128,64]{2,1,0:T(8,128)(2,1)S(1)} %slice.29, bf16[8,128,512]{2,1,0:T(8,128)(2,1)} %convolution_convert_fusion, bf16[768,576]{0,1:T(8,128)(2,1)S(1)} %copy.33, bf16[256,576]{0,1:T(8,128)(2,1)S(1)} %copy.32, ...), kind=kOutput, calls=%fused_computation.48 | convolution fusion | flops 1372374144 | bytes 5017600 | tf_op jit(solution)/shard_map/sub | solution.py:709
  35.6 1.0 pad_maximum_fusion
  36.6 3.8 %fusion.14 = bf16[8,128,128]{1,2,0:T(8,128)(2,1)S(1)} fusion(bf16[8,512,128]{2,1,0:T(8,128)(2,1)} %param.27, bf16[8,128,1152]{2,1,0:T(8,128)(2,1)} %get-tuple-element.9, bf16[1152,576]{0,1:T(8,128)(2,1)S(1)} %pad_maximum_fusion, f32[8,128]{1,0:T(8,128)} %get-tuple-element.8), kind=kOutput, calls=%fused_computation.15 | convolution fusion | flops 1343356928 | bytes 4853760 | tf_op jit(solution)/shard_map/htr,hrv->thv/dot_general | solution.py:717
  40.5 0.0 copy-start.2
  40.5 0.0 copy-start.3
  40.5 3.9 %fusion.34.projected = f32[128,2048]{1,0:T(8,128)} fusion(bf16[128,1024]{0,1:T(8,128)(2,1)S(1)} %bitcast.44, bf16[1024,2048]{1,0:T(8,128)(2,1)} %param.28), kind=kOutput, calls=%fused_computation.49 | convolution fusion | flops 536870912 | bytes 5505024 | tf_op jit(solution)/shard_map/dot_general | solution.py:720
  44.4 0.0 copy-done.2
  44.4 0.1 fusion.17
  44.6 0.2 select_reduce_fusion
  44.8 1.3 reshape.37.slot_weight
  46.1 0.8 fusion.20.chooser
  46.9 0.0 copy-done.3
  46.9 0.6 broadcast_in_dim.99.gain
  47.5 141.6 %shard_map.186 = (bf16[128,1024]{1,0:T(8,128)(2,1)}, bf16[128,1024]{1,0:T(8,128)(2,1)}) custom-call(f32[128,2048]{1,0:T(8,128)} %fusion.34.projected, bf16[128,1024]{1,0:T(8,128)(2,1)} %residual.1, bf16[1,1024]{1,0:T(2,128)(2,1)} %broadcast_in_dim.99.gain, bf16[16,64,128]{2,1,0:T(8,128)(2,1)} %fusion.20.chooser, f32[1024,1]{1,0:T(8,128)} %reshape.37.slot_weight, ...), custom_call_target="tpu_custom_call" | custom-call | tf_op jit(solution)/shard_map/pallas_call | solution.py:610
  189.1 1.7 copy.47
  190.8 1.7 copy.48
  (9 shorter events, 0.2 us)
Async XLA Ops:
  0.6 25.2 %copy-start = (bf16[8,128,512]{2,1,0:T(8,128)(2,1)S(1)}, bf16[8,128,512]{2,1,0:T(8,128)(2,1)}, u32[]{:S(2)}) copy-start(bf16[8,128,512]{2,1,0:T(8,128)(2,1)} %param.26) | copy-start | bytes 3145732
  24.5 4.2 %copy-start.1 = (bf16[128,576]{0,1:T(8,128)(2,1)S(1)}, bf16[128,576]{0,1:T(8,128)(2,1)}, u32[]{:S(2)}) copy-start(bf16[128,576]{0,1:T(8,128)(2,1)} %param.19) | copy-start | bytes 442372
  40.5 4.0 %copy-start.2 = (f32[16,1,128]{2,1,0:T(1,128)S(1)}, f32[16,1,128]{2,1,0:T(1,128)}, u32[]{:S(2)}) copy-start(f32[16,1,128]{2,1,0:T(1,128)} %get-tuple-element.5) | copy-start | bytes 24580
  40.5 6.4 %copy-start.3 = (bf16[1024]{0:T(1024)(128)(2,1)S(1)}, bf16[1024]{0:T(1024)(128)(2,1)}, u32[]{:S(2)}) copy-start(bf16[1024]{0:T(1024)(128)(2,1)} %param.30) | copy-start | bytes 6148

commit v4 on v3

--- a/solution.py
+++ b/solution.py
@@ -286,7 +286,7 @@
     pl.semaphore_wait(barrier, 3 + (1 - z // 3) + (z + 2) // 3)
 
 
-def spread_tokens(whole, send, recv, finish):
+def spread_tokens(whole, send, recv):
     z, x, core, y = coordinates()
     half_rows, half_cols = whole.shape[1] // 2, whole.shape[2] // 2
 
@@ -344,38 +344,39 @@
                 hop(zp, 1 - x, 1 - y, half, core, 2, over_x).wait_recv()
                 copy.start()
 
+    def each(distance, work):
+        if distance == 0:
+            work(z)
+            return
+
+        @pl.when(z + distance < 4)
+        def _():
+            work(z + distance)
+
+        @pl.when(z - distance >= 0)
+        def _():
+            work(z - distance)
+
     def arrive(zp):
         for half in range(2):
             hop(zp, x, y, half, core, 0, over_x).wait_recv()
         column(zp, False)
 
-    def ready(zp):
+    column(z, False)
+    for distance in range(1, 4):
+        each(distance, arrive)
+        each(distance - 1, lambda zp: beside(zp, False))
+        if distance > 1:
+            each(distance - 2, lambda zp: diagonal(zp, False))
+    each(3, lambda zp: beside(zp, False))
+    each(2, lambda zp: diagonal(zp, False))
+    each(3, lambda zp: diagonal(zp, False))
+
+    def close(zp, carry):
         for xp in range(2):
             for yp in range(2):
                 for half in range(2):
                     hop(zp, xp, yp, half, 1 - core, 4, other).wait_recv()
-        finish(zp)
-
-    column(z, False)
-
-    def turn(step, carry):
-        for lag, work, first in (
-            (0, arrive, 1), (2, lambda zp: beside(zp, False), 0),
-            (4, lambda zp: diagonal(zp, False), 0), (5, ready, 0),
-        ):
-            item = step - lag
-            distance = (item + 1) // 2
-            zp = z + distance * (2 * (item % 2) - 1)
-
-            @pl.when((item >= first) & (item < 7) & (zp >= 0) & (zp < 4))
-            def _(work=work, zp=zp):
-                work(zp)
-
-        return carry
-
-    lax.fori_loop(1, 12, turn, 0)
-
-    def close(zp, carry):
         column(zp, True)
         beside(zp, True)
         diagonal(zp, True)
@@ -384,15 +385,7 @@
     lax.fori_loop(0, 4, close, 0)
 
 
-def core_hop(acc, core_in, sems, zp, xp):
-    z, x, core, y = coordinates()
-    return pltpu.make_async_remote_copy(
-        acc.at[zp, xp * 2 + 1 - core], core_in.at[zp, xp], sems.at[0, xp, zp], sems.at[1, xp, zp],
-        device_id=place(z, x, 1 - core, y), device_id_type=MESH,
-    )
-
-
-def return_sums(acc, core_in, x_diag, y_diag, x_in, y_in, up_in, down_in, sems):
+def return_sums(compute, acc, core_in, x_diag, y_diag, x_in, y_in, up_in, down_in, sems):
     z, x, core, y = coordinates()
     rows, half_cols = acc.shape[2], acc.shape[3] // 2
     half_rows = rows // 2
@@ -412,7 +405,7 @@
         return acc.at[zp, xp * 2 + cp]
 
     def core_copy(zp, xp):
-        return core_hop(acc, core_in, sems, zp, xp)
+        return copy(block(zp, xp, 1 - core), core_in.at[zp, xp], xp, zp, other)
 
     def diag_copies(zp):
         far = block(zp, 1 - x, core)
@@ -492,19 +485,26 @@
     def stage(step, carry):
         @pl.when(step < 4)
         def _():
-            cores(turn(step))
+            zp = turn(step)
+            compute(zp)
+            for xp in range(2):
+                core_copy(zp, xp).start()
 
         @pl.when((step >= 1) & (step < 5))
         def _():
-            corners(turn(step - 1))
-
-        @pl.when(step >= 2)
-        def _():
-            columns(turn(step - 2))
+            cores(turn(step - 1))
+
+        @pl.when((step >= 2) & (step < 6))
+        def _():
+            corners(turn(step - 2))
+
+        @pl.when(step >= 3)
+        def _():
+            columns(turn(step - 3))
 
         return carry
 
-    lax.fori_loop(0, 6, stage, 0)
+    lax.fori_loop(0, 7, stage, 0)
 
     def close(zp, carry):
         for xp in range(2):
@@ -567,6 +567,7 @@
     both = sums + squares_in[:, :1]
     scaled = stream * lax.rsqrt(both / (2 * half_cols) + EPSILON) * gain[...].astype(jnp.float32)
     whole[(z * 2 + x) * 2 + core, :, mine] = scaled.astype(jnp.bfloat16)
+    spread_tokens(whole, send, recv)
     for load in loads:
         load.wait()
     capacity = chooser.shape[1]
@@ -590,11 +591,7 @@
                 (((0,), (0,)), ((), ())), preferred_element_type=jnp.float32,
             ).astype(jnp.bfloat16)
 
-        for xp in range(2):
-            core_hop(acc, core_in, sems, zp, xp).start()
-
-    spread_tokens(whole, send, recv, compute)
-    own = return_sums(acc, core_in, x_diag, y_diag, x_in, y_in, up_in, down_in, sems)
+    own = return_sums(compute, acc, core_in, x_diag, y_diag, x_in, y_in, up_in, down_in, sems)
     mixed[...] = (attended[...].astype(jnp.float32) + own[...].astype(jnp.float32)).astype(jnp.bfloat16)
 
 

time: 194 us -> 185 us (0.954)
  Pallas kernels: 156 us -> 148 us
    pallas_call x1, Pallas kernels: 142 us -> 133 us  [run_experts(): pl.pallas_call(expert_kernel, out_shape=(jax.ShapeDtypeStruct((tokens, ha...]
where the time goes in v4:
time: 185 us; the launch traced here: 184 us
  Pallas kernels  148 us (80%)
  matrix products  16.1 us (9%)
  local copies, waits for them, and re-layouts  9.65 us (5%)
  other arithmetic  7.48 us (4%)
  between operations  2.78 us (2%)
    pallas_call x1, Pallas kernels, run_experts(): pl.pallas_call(expert_kernel, out_shape=(jax.ShapeDtypeStruct((tokens, ha...  133 us
    pallas_call x1, Pallas kernels, share_prompts(): pl.pallas_call(prompt_kernel, out_shape=(jax.ShapeDtypeStruct((groups, ro...  14.9 us
    sub x1, matrix products, on_block(): weights = jnp.exp(scores - jnp.max(scores, axis=2, keepdims=True))  6.82 us
    unnamed x12, local copies, waits for them, and re-layouts  4.61 us
    dot_general x1, matrix products, on_block(): jnp.dot(heads_out.reshape(tokens, -1), out_weight, preferred_element_type...  3.94 us
    dot_general x1, matrix products, on_block(): jnp.einsum('htr,hrv->thv', latent, value_weight, preferred_element_type=j...  3.81 us

profile of v4, /device:TPU:8, one launch (start us, length us, event | category | flops | bytes accessed | tf_op | source)
XLA Modules:
  0.0 184.3 jit_solution(12584448805886020837)
XLA Ops:
  0.6 0.0 copy-start
  0.6 1.4 fusion.24
  2.7 1.3 fusion.28
  5.4 0.8 select_reduce_fusion.2
  6.2 0.7 add_compare_fusion
  6.9 0.1 lt.19
  7.1 1.3 select_reduce_fusion.1
  8.4 14.9 %shard_map.185 = (bf16[2,256,576]{2,1,0:T(8,128)(2,1)}, f32[16,1,128]{2,1,0:T(1,128)}) custom-call(bf16[2,16,576]{2,1,0:T(8,128)(2,1)} %block_ref.1, f32[16,1,128]{2,1,0:T(1,128)} %bitcast.47), custom_call_target="tpu_custom_call" | custom-call | tf_op jit(solution)/shard_map/pallas_call | solution.py:259
  23.2 1.1 select_bitcast_fusion
  24.4 0.2 copy.32
  24.5 0.0 copy-start.1
  24.5 1.2 copy.31
  25.8 0.0 copy-done
  25.8 1.4 convolution_convert_fusion
  27.2 1.5 copy.33
  28.8 0.0 copy-done.1
  28.8 6.8 %fusion.29 = (f32[8,128]{1,0:T(8,128)}, bf16[8,128,1152]{2,1,0:T(8,128)(2,1)}) fusion(pred[128,1152]{1,0:T(8,128)(4,1)S(1)} %pad_add_fusion, bf16[8,128,64]{2,1,0:T(8,128)(2,1)S(1)} %slice.29, bf16[8,128,512]{2,1,0:T(8,128)(2,1)} %convolution_convert_fusion, bf16[768,576]{0,1:T(8,128)(2,1)S(1)} %copy.33, bf16[256,576]{0,1:T(8,128)(2,1)S(1)} %copy.32, ...), kind=kOutput, calls=%fused_computation.48 | convolution fusion | flops 1372374144 | bytes 5017600 | tf_op jit(solution)/shard_map/sub | solution.py:706
  35.6 1.0 pad_maximum_fusion
  36.6 3.8 %fusion.14 = bf16[8,128,128]{1,2,0:T(8,128)(2,1)S(1)} fusion(bf16[8,512,128]{2,1,0:T(8,128)(2,1)} %param.27, bf16[8,128,1152]{2,1,0:T(8,128)(2,1)} %get-tuple-element.9, bf16[1152,576]{0,1:T(8,128)(2,1)S(1)} %pad_maximum_fusion, f32[8,128]{1,0:T(8,128)} %get-tuple-element.8), kind=kOutput, calls=%fused_computation.15 | convolution fusion | flops 1343356928 | bytes 4853760 | tf_op jit(solution)/shard_map/htr,hrv->thv/dot_general | solution.py:714
  40.5 0.0 copy-start.2
  40.5 0.0 copy-start.3
  40.5 3.9 %fusion.34.projected = f32[128,2048]{1,0:T(8,128)} fusion(bf16[128,1024]{0,1:T(8,128)(2,1)S(1)} %bitcast.44, bf16[1024,2048]{1,0:T(8,128)(2,1)} %param.28), kind=kOutput, calls=%fused_computation.49 | convolution fusion | flops 536870912 | bytes 5505024 | tf_op jit(solution)/shard_map/dot_general | solution.py:717
  44.4 0.0 copy-done.2
  44.4 0.1 fusion.17
  44.6 0.2 select_reduce_fusion
  44.8 1.3 reshape.37.slot_weight
  46.1 0.8 fusion.20.chooser
  46.9 0.0 copy-done.3
  46.9 0.6 broadcast_in_dim.99.gain
  47.5 133.4 %shard_map.186 = (bf16[128,1024]{1,0:T(8,128)(2,1)}, bf16[128,1024]{1,0:T(8,128)(2,1)}) custom-call(f32[128,2048]{1,0:T(8,128)} %fusion.34.projected, bf16[128,1024]{1,0:T(8,128)(2,1)} %residual.1, bf16[1,1024]{1,0:T(2,128)(2,1)} %broadcast_in_dim.99.gain, bf16[16,64,128]{2,1,0:T(8,128)(2,1)} %fusion.20.chooser, f32[1024,1]{1,0:T(8,128)} %reshape.37.slot_weight, ...), custom_call_target="tpu_custom_call" | custom-call | tf_op jit(solution)/shard_map/pallas_call | solution.py:607
  181.0 1.7 copy.47
  182.6 1.7 copy.48
  (9 shorter events, 0.2 us)
Async XLA Ops:
  0.6 25.2 %copy-start = (bf16[8,128,512]{2,1,0:T(8,128)(2,1)S(1)}, bf16[8,128,512]{2,1,0:T(8,128)(2,1)}, u32[]{:S(2)}) copy-start(bf16[8,128,512]{2,1,0:T(8,128)(2,1)} %param.26) | copy-start | bytes 3145732
  24.5 4.2 %copy-start.1 = (bf16[128,576]{0,1:T(8,128)(2,1)S(1)}, bf16[128,576]{0,1:T(8,128)(2,1)}, u32[]{:S(2)}) copy-start(bf16[128,576]{0,1:T(8,128)(2,1)} %param.19) | copy-start | bytes 442372
  40.5 4.0 %copy-start.2 = (f32[16,1,128]{2,1,0:T(1,128)S(1)}, f32[16,1,128]{2,1,0:T(1,128)}, u32[]{:S(2)}) copy-start(f32[16,1,128]{2,1,0:T(1,128)} %get-tuple-element.5) | copy-start | bytes 24580
  40.5 6.4 %copy-start.3 = (bf16[1024]{0:T(1024)(128)(2,1)S(1)}, bf16[1024]{0:T(1024)(128)(2,1)}, u32[]{:S(2)}) copy-start(bf16[1024]{0:T(1024)(128)(2,1)} %param.30) | copy-start | bytes 6148
